TPU v7x, 32 devices: a whole 2x2x4 slice. The times are simulated.
32 devices in a mesh: dp: 8 (over y, x, core), group: 4 (over z).
Axes of the slice: x: 2, y: 2, z: 4, core: 2. Of those that a mesh axis runs over, the one named last changes fastest.
Arguments:
- tokens: bfloat16 [8192, 640], P(('dp', 'group')), may hold values from -6 to 6
- cotangent: bfloat16 [8192, 640], P(('dp', 'group')), may hold values from -6 to 6
- positions: int32 [8192], P(('dp', 'group')), may hold values from 0 to 511, as said below
- attn_weights: float32 [12832, 128], P(('dp', 'group'))
- ffn_weights: float32 [30752, 128], P(('dp', 'group'))
- attn_m: float32 [12832, 128], P(('dp', 'group')), may hold values from -28 to 28
- attn_v: float32 [12832, 128], P(('dp', 'group')), may hold values from 9 to 82
- ffn_m: float32 [30752, 128], P(('dp', 'group')), may hold values from -28 to 28
- ffn_v: float32 [30752, 128], P(('dp', 'group')), may hold values from 9 to 82
Outputs:
- output: bfloat16 [8192, 640], P(('dp', 'group'))
- grad_tokens: float32 [8192, 640], P(('dp', 'group'))
- attn_grad: float32 [12832, 128], P(('dp', 'group'))
- ffn_grad: float32 [30752, 128], P(('dp', 'group'))
- attn_new: float32 [12832, 128], P(('dp', 'group'))
- ffn_new: float32 [30752, 128], P(('dp', 'group'))
- attn_m_new: float32 [12832, 128], P(('dp', 'group'))
- attn_v_new: float32 [12832, 128], P(('dp', 'group'))
- ffn_m_new: float32 [30752, 128], P(('dp', 'group'))
- ffn_v_new: float32 [30752, 128], P(('dp', 'group'))
Inputs may be any that keep to these rules, and one draw needn't show every extreme that they name: Tokens come in sequences laid end to end; a token's position counts from its sequence's first token, so positions rise by one along a sequence. Each block of 1024 tokens along one group holds whole sequences, and every such block holds one sequence of exactly 512 tokens.
All inputs are finite; a program needn't handle non-finite values.
Results may differ from a plain program's by a relative error of at most 0.015.
The roundings to bfloat16 on the way count: a program that leaves them out, or rounds other values in their place, can miss the bound.
Values may be sent and summed in bfloat16 or wider, within the bound.
No kernel may reach another device: no remote copies, remote signals or barrier semaphores. Data moves between devices by JAX's collectives and lax.ppermute only.
A program may use at most 128 MiB of HBM per device.

v0:
```python
import functools
import math

import jax
import jax.numpy as jnp
from jax import lax
from jax.experimental import pallas as pl
from jax.experimental.pallas import tpu as pltpu
from jax.sharding import PartitionSpec as P


D = 640
H = 4
HD = 256
FF = 2048
WINDOW = 512
STEP = 3


NORM_EPS = 1e-06
THETA = 10000.0
BETA_ONE = 0.9
BETA_TWO = 0.95
LEARN_RATE = 0.02
WEIGHT_DECAY = 0.1
ADAM_EPS = 1e-08
GELU_COEF = 0.7978845608028654


def passed_along(shard, axis, by):
    count = lax.axis_size(axis)
    pairs = [(i, i + by) for i in range(count) if 0 <= i + by < count]
    return lax.ppermute(shard, axis, pairs)


def attn_shapes():
    return [(D, H * HD), (D, HD), (D, HD), (H * HD, D), (D,), (HD,), (HD,), (D,)]


def ffn_shapes():
    return [(D, FF), (D, FF), (FF, D), (D,), (D,)]


def rope_tables(positions):
    half_dim = HD // 2
    freqs = jnp.power(THETA, -2.0 * jnp.arange(half_dim, dtype=jnp.float32) / HD)
    angles = positions.astype(jnp.float32)[:, None] * freqs[None, :]
    return (jnp.cos(angles), jnp.sin(angles))


def gelu_pair(values):
    tangent = jnp.tanh(GELU_COEF * (values + 0.044715 * (values * values * values)))
    activated = 0.5 * values * (1.0 + tangent)
    slope_v = 0.5 * (1.0 + tangent) + 0.5 * values * (1.0 - tangent * tangent) * GELU_COEF * (
        1.0 + 3.0 * 0.044715 * values * values
    )
    return (activated, slope_v)


def times_trans(left, right):
    return lax.dot_general(
        left, right, (((1,), (1,)), ((), ())), preferred_element_type=jnp.float32
    )


def adam_step(param, grad_in, moment_one, moment_two):
    new_one = BETA_ONE * moment_one + (1.0 - BETA_ONE) * grad_in
    new_two = BETA_TWO * moment_two + (1.0 - BETA_TWO) * grad_in * grad_in
    corr_one = new_one / (1.0 - BETA_ONE**STEP)
    corr_two = new_two / (1.0 - BETA_TWO**STEP)
    new_param = param - LEARN_RATE * (
        corr_one / (jnp.sqrt(corr_two) + ADAM_EPS) + WEIGHT_DECAY * param
    )
    return (new_param, new_one, new_two)


BF = jnp.bfloat16
F32 = jnp.float32
VMEM_LIMIT = 60 * 1024 * 1024


def rows_up(count, unit=16):
    return -(-count // unit) * unit


def lay_out(jobs, lefts, rights, gains, flat):
    offset = 0
    tile = 128
    for (m, n), left, right in zip(jobs, lefts, rights):
        per_row = n // 128
        skip = left.shape[0] - right.shape[0]

        def step(i, carry, left=left, right=right, per_row=per_row, offset=offset, skip=skip):
            start = pl.multiple_of(i * tile, tile)
            block = contract(left[skip:, pl.ds(start, tile)], right[...], 0, 0)
            base = offset + i * (tile * per_row)
            for j in range(per_row):
                flat[pl.ds(base + j, tile, stride=per_row), :] = block[:, 128 * j : 128 * j + 128]
            return carry

        lax.fori_loop(0, m // tile, step, 0)
        offset = offset + m * per_row
    tail = flat.shape[0] - offset
    flat[pl.ds(offset, tail), :] = jnp.zeros((tail, 128), F32)
    for row in gains:
        for j in range(row.shape[1] // 128):
            flat[pl.ds(offset, 1), :] = row[:, 128 * j : 128 * j + 128]
            offset = offset + 1


def halves(padded):
    cut = padded // 32 * 16
    return (cut, padded - cut)


def cut_owners(flat, own, padded, sizes, core, outs):
    slow, fast, _, depth = sizes
    cut = halves(padded)[0]

    def step(i, carry):
        lead, z = i // depth, i % depth
        for which, (head, rest) in ((1 - core, outs[:2]), (core, outs[2:])):
            start = ((lead * 2 + which) * depth + z) * own
            block = flat[pl.ds(start, padded), :].astype(BF)
            head[i] = block[:cut]
            rest[i] = block[cut:]
        return carry

    lax.fori_loop(0, slow * fast * depth, step, 0)


def pack_body(jobs, own, padded, sizes, core_ref, *refs):
    count = len(jobs)
    lefts, rights, gains = refs[:count], refs[count : 2 * count], refs[2 * count : -5]
    outs, flat = refs[-5:-1], refs[-1]
    lay_out(jobs, lefts, rights, gains, flat)
    cut_owners(flat, own, padded, sizes, core_ref[0], outs)


def pack_grads(jobs, lefts, rights, gains, own, sizes, core):
    padded = rows_up(own)
    devices = math.prod(sizes)
    half = devices // 2
    whole = rows_up(devices * own + 16, 8)
    out = tuple(jax.ShapeDtypeStruct((half, rows, 128), BF) for rows in halves(padded)) * 2
    vmem = pl.BlockSpec(memory_space=pltpu.VMEM)
    flops = sum(2 * m * n * lefts[0].shape[0] for m, n in jobs)
    return pl.pallas_call(
        functools.partial(pack_body, jobs, own, padded, sizes),
        out_shape=out,
        in_specs=[pl.BlockSpec(memory_space=pltpu.SMEM)] + [vmem] * (2 * len(jobs) + len(gains)),
        out_specs=(vmem,) * 4,
        scratch_shapes=[pltpu.VMEM((whole, 128), F32)],
        compiler_params=pltpu.CompilerParams(vmem_limit_bytes=VMEM_LIMIT),
        cost_estimate=pl.CostEstimate(
            flops=flops, bytes_accessed=devices * padded * 256, transcendentals=0
        ),
    )(core, *lefts, *rights, *gains)


def spread(flat, dims_list, outs):
    offset = 0
    tile = 128
    for (m, n), out in zip(dims_list, outs):
        per_row = n // 128

        def step(i, carry, out=out, per_row=per_row, offset=offset):
            start = pl.multiple_of(i * tile, tile)
            base = offset + i * (tile * per_row)
            for j in range(per_row):
                piece = flat[pl.ds(base + j, tile, stride=per_row), :]
                out[pl.ds(start, tile), 128 * j : 128 * j + 128] = piece.astype(BF)
            return carry

        lax.fori_loop(0, m // tile, step, 0)
        offset = offset + m * per_row
    if len(outs) > len(dims_list):
        outs[-1][...] = flat[pl.ds(offset, outs[-1].shape[0]), :]
    return offset


def unpack_pieces_body(dims_list, own, sizes, at_ref, *refs):
    first, first_far, second, second_far = refs[:4]
    outs, flat = refs[4:-1], refs[-1]
    slow, fast, _, depth = sizes
    head = first.shape[1]
    near = tuple(at_ref[i] for i in range(3))

    def seen(extent, owner, here):
        return owner ^ here if extent == 2 else owner

    def put(i, carry):
        z, b, a = i % depth, (i // depth) % fast, i // (depth * fast)
        ra, rb = seen(slow, a, near[0]), seen(fast, b, near[1])
        one = (ra * fast + rb) * depth + z
        two = (rb * slow + ra) * depth + z
        for core, left, right in ((near[2], first, second), (1 - near[2], first_far, second_far)):
            base = (((a * fast + b) * 2 + core) * depth + z) * own
            flat[pl.ds(base, head), :] = left[one].astype(F32)
            flat[pl.ds(base + head, own - head), :] = right[two, : own - head].astype(F32)
        return carry

    lax.fori_loop(0, slow * fast * depth, put, 0)
    spread(flat, dims_list, outs)


def unpack(body, dims_list, gain_rows, own, devices, ins, scalars=()):
    vmem = pl.BlockSpec(memory_space=pltpu.VMEM)
    outs = [jax.ShapeDtypeStruct(dims, BF) for dims in dims_list]
    outs.append(jax.ShapeDtypeStruct((rows_up(gain_rows, 8), 128), F32))
    return pl.pallas_call(
        body,
        out_shape=tuple(outs),
        in_specs=[pl.BlockSpec(memory_space=pltpu.SMEM)] * len(scalars) + [vmem] * len(ins),
        out_specs=tuple([vmem] * len(outs)),
        scratch_shapes=[pltpu.VMEM((rows_up(devices * own + 8, 8), 128), F32)],
        compiler_params=pltpu.CompilerParams(vmem_limit_bytes=VMEM_LIMIT),
        cost_estimate=pl.CostEstimate(
            flops=0, bytes_accessed=devices * own * 512, transcendentals=0
        ),
    )(*scalars, *ins)


def contract(left, right, left_dim, right_dim):
    return lax.dot_general(
        left, right, (((left_dim,), (right_dim,)), ((), ())), preferred_element_type=F32
    )


def row_norm(values):
    return lax.rsqrt(jnp.mean(values * values, axis=-1, keepdims=True) + NORM_EPS)


def turn(values, cosine, sine_t, sign):
    first, second = values[:, : HD // 2], values[:, HD // 2 :]
    return jnp.concatenate(
        [first * cosine - sign * (second * sine_t), second * cosine + sign * (first * sine_t)],
        axis=-1,
    )


def seen_keys(reach, place, own, window):
    gap = lax.broadcasted_iota(jnp.int32, (own, window), 0) + (window - own)
    gap = gap - lax.broadcasted_iota(jnp.int32, (own, window), 1)
    return (gap >= 0) & (gap <= jnp.minimum(place, reach - 1))


def norm_grad(values, recip, gain, grad_out):
    scaled = grad_out * (1.0 + gain)
    grad_in = recip * scaled - values * recip * recip * recip * jnp.mean(
        scaled * values, axis=-1, keepdims=True
    )
    return grad_in, jnp.sum(grad_out * values * recip, axis=0, keepdims=True)


def attention_body(
    tokens, place, cosine, sine_t, w_q, w_k, w_v, w_o, g_in, g_q, g_k, g_mid,
    normed_b, queries, keys, query_b, key_b, value_b, attended_b, branch, middle,
):
    window, own = tokens.shape[0], place.shape[0]
    start = window - own
    values = tokens[...].astype(F32)
    normed_b[...] = (values * row_norm(values) * (1.0 + g_in[...])).astype(BF)
    keys[...] = contract(normed_b[...], w_k[...], 1, 0)
    value_b[...] = contract(normed_b[...], w_v[...], 1, 0).astype(BF)
    keyed = keys[...]
    keyed = keyed * row_norm(keyed) * (1.0 + g_k[...])
    key_b[...] = turn(keyed, cosine[...], sine_t[...], 1.0).astype(BF)
    queries[...] = contract(normed_b[start:, :], w_q[...], 1, 0)

    def head(h, carry):
        at = pl.ds(pl.multiple_of(h * HD, HD), HD)
        asked = queries[:, at]
        asked = asked * row_norm(asked) * (1.0 + g_q[...])
        asked = turn(asked, cosine[start:, :], sine_t[start:, :], 1.0) * (HD ** (-0.5))
        query_b[:, at] = asked.astype(BF)
        visible = seen_keys(WINDOW, place[...], own, window)
        scores = contract(query_b[:, at], key_b[...], 1, 1)
        total = jnp.sum(jnp.where(visible, jnp.exp(scores), 0.0), axis=-1, keepdims=True)
        prob = jnp.where(visible, jnp.exp(scores - jnp.log(total)), 0.0)
        attended_b[:, at] = contract(prob.astype(BF), value_b[...], 1, 0).astype(BF)
        return carry

    lax.fori_loop(0, H, head, 0)
    branch[...] = contract(attended_b[...], w_o[...], 1, 0)
    out = branch[...]
    middle[...] = values[start:, :] + out * row_norm(out) * (1.0 + g_mid[...])


def attention_back_body(
    grad_middle, branch, tokens, place, cosine, sine_t, queries, keys, query_b, key_b, value_b,
    w_q, w_k, w_v, w_o, g_in, g_q, g_k, g_mid,
    grad_branch_b, grad_q_b, grad_k_b, grad_v_b, grad_normed, sum_in, sum_q, sum_k, sum_mid,
    grad_key, grad_value,
):
    window, own = tokens.shape[0], place.shape[0]
    start = window - own
    out = branch[...]
    grad_branch, sum_mid[...] = norm_grad(out, row_norm(out), g_mid[...], grad_middle[...])
    grad_branch_b[...] = grad_branch.astype(BF)
    grad_key[...] = jnp.zeros_like(grad_key)
    grad_value[...] = jnp.zeros_like(grad_value)
    sum_q[...] = jnp.zeros_like(sum_q)

    def head(h, carry):
        at = pl.ds(pl.multiple_of(h * HD, HD), HD)
        grad_att = contract(grad_branch_b[...], w_o[at, :], 1, 1).astype(BF)
        visible = seen_keys(WINDOW, place[...], own, window)
        scores = contract(query_b[:, at], key_b[...], 1, 1)
        total = jnp.sum(jnp.where(visible, jnp.exp(scores), 0.0), axis=-1, keepdims=True)
        prob = jnp.where(visible, jnp.exp(scores - jnp.log(total)), 0.0)
        grad_prob = contract(grad_att, value_b[...], 1, 1)
        row_dot = jnp.sum(prob * grad_prob, axis=-1, keepdims=True)
        grad_score = (prob * (grad_prob - row_dot)).astype(BF)
        grad_query = contract(grad_score, key_b[...], 1, 0)
        grad_key[...] += contract(grad_score, query_b[:, at], 0, 0)
        grad_value[...] += contract(prob.astype(BF), grad_att, 0, 0)
        back = turn(grad_query * (HD ** (-0.5)), cosine[start:, :], sine_t[start:, :], -1.0)
        asked = queries[:, at]
        grad_q, part = norm_grad(asked, row_norm(asked), g_q[...], back)
        grad_q_b[:, at] = grad_q.astype(BF)
        sum_q[...] += part
        return carry

    lax.fori_loop(0, H, head, 0)
    keyed = keys[...]
    back = turn(grad_key[...], cosine[...], sine_t[...], -1.0)
    grad_k, sum_k[...] = norm_grad(keyed, row_norm(keyed), g_k[...], back)
    grad_k_b[...] = grad_k.astype(BF)
    grad_v_b[...] = grad_value[...].astype(BF)
    grad_normed[...] = contract(grad_q_b[...], w_q[...], 1, 1)
    through = contract(grad_k_b[...], w_k[...], 1, 1) + contract(grad_v_b[...], w_v[...], 1, 1)
    values = tokens[...].astype(F32)
    scaled = values * row_norm(values)
    sum_in[...] = jnp.sum(through * scaled, axis=0, keepdims=True) + jnp.sum(
        grad_normed[...] * scaled[start:, :], axis=0, keepdims=True
    )


def in_vmem(body, outs, scratch, flops, args):
    vmem = pl.BlockSpec(memory_space=pltpu.VMEM)
    out_shape = tuple(jax.ShapeDtypeStruct(shape, kind) for shape, kind in outs)
    moved = sum(math.prod(o.shape) * o.dtype.itemsize for o in (*out_shape, *args))
    return pl.pallas_call(
        body,
        out_shape=out_shape,
        in_specs=[vmem] * len(args),
        out_specs=tuple([vmem] * len(outs)),
        scratch_shapes=[pltpu.VMEM(shape, F32) for shape in scratch],
        compiler_params=pltpu.CompilerParams(vmem_limit_bytes=VMEM_LIMIT),
        cost_estimate=pl.CostEstimate(flops=flops, bytes_accessed=moved, transcendentals=0),
    )(*args)


def attention(tokens, place, cosine, sine_t, weights):
    window, own = tokens.shape[0], place.shape[0]
    outs = [
        ((window, D), BF), ((own, H * HD), F32), ((window, HD), F32), ((own, H * HD), BF),
        ((window, HD), BF), ((window, HD), BF), ((own, H * HD), BF), ((own, D), F32), ((own, D), F32),
    ]
    flops = 4 * own * window * H * HD + 4 * own * D * H * HD + 4 * window * D * HD
    return in_vmem(attention_body, outs, (), flops, (tokens, place, cosine, sine_t, *weights))


def attention_back(grad_middle, branch, tokens, place, cosine, sine_t, kept, weights):
    window, own = tokens.shape[0], place.shape[0]
    outs = [
        ((own, D), BF), ((own, H * HD), BF), ((window, HD), BF), ((window, HD), BF), ((own, D), F32),
        ((1, D), F32), ((1, HD), F32), ((1, HD), F32), ((1, D), F32),
    ]
    flops = 10 * own * window * H * HD + 4 * own * D * H * HD + 4 * window * D * HD
    args = (grad_middle, branch, tokens, place, cosine, sine_t, *kept, *weights)
    return in_vmem(attention_back_body, outs, ((window, HD), (window, HD)), flops, args)


def feed_forward_body(
    dims_list, own_rows, padded, sizes,
    core_ref, middle, top_in, blocks,
    output, grad_middle, send_head, send_rest, keep_head, keep_rest,
    flat, w_g, w_u, w_d, pre_b, hidden_b, grad_ffn_b, grad_gate_b, grad_upper_b, gate, upper, total,
):
    def put(d, carry):
        flat[pl.ds(d * own_rows, own_rows), :] = blocks[d].astype(F32)
        return carry

    lax.fori_loop(0, blocks.shape[0], put, 0)
    offset = spread(flat, dims_list, (w_g, w_u, w_d))
    rows = D // 128
    g_pre, g_post = (
        jnp.concatenate([flat[pl.ds(at + j, 1), :] for j in range(rows)], axis=1)
        for at in (offset, offset + rows)
    )
    tile = 512
    steps = gate.shape[1] // tile
    values = middle[...]
    recip = row_norm(values)
    pre_b[...] = (values * recip * (1.0 + g_pre)).astype(BF)
    total[...] = jnp.zeros_like(total)

    def forward(t, carry):
        at = pl.ds(pl.multiple_of(t * tile, tile), tile)
        gate_t = contract(pre_b[...], w_g[:, at], 1, 0)
        upper_t = contract(pre_b[...], w_u[:, at], 1, 0)
        gate[:, at] = gate_t
        upper[:, at] = upper_t
        activated, _ = gelu_pair(gate_t)
        hidden_b[:, at] = (activated * upper_t).astype(BF)
        total[...] += contract(hidden_b[:, at], w_d[at, :], 1, 0)
        return carry

    lax.fori_loop(0, steps, forward, 0)
    ffn_out = total[...]
    recip_post = row_norm(ffn_out)
    output[...] = (values + ffn_out * recip_post * (1.0 + g_post)).astype(BF)
    top = top_in[...].astype(F32)
    grad_ffn, sum_post = norm_grad(ffn_out, recip_post, g_post, top)
    grad_ffn_b[...] = grad_ffn.astype(BF)
    total[...] = jnp.zeros_like(total)

    def backward(t, carry):
        at = pl.ds(pl.multiple_of(t * tile, tile), tile)
        grad_hidden = contract(grad_ffn_b[...], w_d[at, :], 1, 1)
        activated, slope = gelu_pair(gate[:, at])
        grad_gate_b[:, at] = (grad_hidden * upper[:, at] * slope).astype(BF)
        grad_upper_b[:, at] = (grad_hidden * activated).astype(BF)
        total[...] += contract(grad_gate_b[:, at], w_g[:, at], 1, 1)
        total[...] += contract(grad_upper_b[:, at], w_u[:, at], 1, 1)
        return carry

    lax.fori_loop(0, steps, backward, 0)
    grad_add, sum_pre = norm_grad(values, recip, g_pre, total[...])
    grad_middle[...] = top + grad_add
    lay_out(
        dims_list,
        (pre_b, pre_b, hidden_b),
        (grad_gate_b, grad_upper_b, grad_ffn_b),
        (sum_pre, sum_post),
        flat,
    )
    outs = (send_head, send_rest, keep_head, keep_rest)
    cut_owners(flat, own_rows, padded, sizes, core_ref[0], outs)


def feed_forward(core, middle, cotangent, blocks, sizes):
    own = middle.shape[0]
    devices, own_rows = blocks.shape[:2]
    padded = rows_up(own_rows)
    dims_list = ffn_shapes()[:3]
    out = tuple(jax.ShapeDtypeStruct((devices // 2, rows, 128), BF) for rows in halves(padded)) * 2
    vmem = pl.BlockSpec(memory_space=pltpu.VMEM)
    scratch = [((rows_up(devices * own_rows + 16, 8), 128), F32)]
    scratch += [(dims, BF) for dims in dims_list]
    scratch += [((own, D), BF), ((own, FF), BF), ((own, D), BF), ((own, FF), BF), ((own, FF), BF)]
    scratch += [((own, FF), F32), ((own, FF), F32), ((own, D), F32)]
    return pl.pallas_call(
        functools.partial(feed_forward_body, dims_list, own_rows, padded, sizes),
        out_shape=(
            jax.ShapeDtypeStruct((own, D), BF), jax.ShapeDtypeStruct((own, D), F32), *out,
        ),
        in_specs=[pl.BlockSpec(memory_space=pltpu.SMEM)] + [vmem] * 3,
        out_specs=(vmem,) * 6,
        scratch_shapes=[pltpu.VMEM(shape, kind) for shape, kind in scratch],
        compiler_params=pltpu.CompilerParams(vmem_limit_bytes=VMEM_LIMIT),
        cost_estimate=pl.CostEstimate(
            flops=18 * own * D * FF, bytes_accessed=4 * blocks.size, transcendentals=own * FF
        ),
    )(core, middle, cotangent, blocks)


def cut_gains(rows, lengths):
    line = rows.reshape(-1)
    starts = [sum(lengths[:i]) for i in range(len(lengths))]
    return tuple(line[a : a + b].reshape(1, b) for a, b in zip(starts, lengths))


def grid_of():
    pairs = lax.axis_size("dp") // 2
    slow = math.isqrt(pairs)
    fast = pairs // slow
    depth = lax.axis_size("group")
    place = lax.axis_index("dp")
    where = (place // (2 * fast), (place // 2) % fast, place % 2, lax.axis_index("group"))
    return ((slow, fast, 2, depth), where)


def step_along(value, axis, by, sizes, senders=None):
    extent = sizes[axis]
    pairs = []
    if axis == 3:
        for i in range(extent):
            if 0 <= i + by < extent and (senders is None or i in senders):
                pairs.append((i, i + by))
        return lax.ppermute(value, "group", pairs)
    stride = (2 * sizes[1], 2, 1)[axis]
    for i in range(sizes[0] * sizes[1] * 2):
        at = (i // stride) % extent
        if 0 <= at + by < extent and (senders is None or at in senders):
            pairs.append((i, i + by * stride))
    return lax.ppermute(value, "dp", pairs)


def swap_along(value, axis, sizes):
    stride = (2 * sizes[1], 2, 1)[axis]
    count = sizes[0] * sizes[1] * 2
    pairs = [(i, i + stride * (1 - 2 * ((i // stride) % 2))) for i in range(count)]
    return lax.ppermute(value, "dp", pairs)


def gather_axis(value, axis, sizes):
    extent = sizes[axis]
    if extent == 2:
        return jnp.stack([value, swap_along(value, axis, sizes)])
    stride = (2 * sizes[1], 2, 1)[axis]
    count = sizes[0] * sizes[1] * 2
    groups = [
        [i + k * stride for k in range(extent)] for i in range(count) if (i // stride) % extent == 0
    ]
    return lax.all_gather(value, "dp", axis=0, axis_index_groups=groups)


def gather_pieces(line, sizes):
    head = line.shape[1] // 32 * 16
    pieces = []
    for part, order in ((line[:, :head], (1, 0)), (line[:, head:], (0, 1))):
        for axis in order:
            part = gather_axis(part, axis, sizes)
        part = part.reshape(-1, *part.shape[-2:])
        pieces += [part, swap_along(part, 2, sizes)]
    return pieces


def swap_line(value, bit, sizes):
    return lax.ppermute(value, "group", [(i, i ^ bit) for i in range(sizes[3])])


def pick(blocks, index, axis=0):
    return lax.dynamic_index_in_dim(blocks, index, axis=axis, keepdims=False)


def scatter_axis(blocks, axis, sizes, where):
    extent, at = (sizes[axis], where[axis])
    if extent == 1:
        return blocks[0].astype(jnp.float32)
    if extent == 2 and axis < 3:
        arrived = swap_along(pick(blocks, 1 - at), axis, sizes)
        return pick(blocks, at).astype(jnp.float32) + arrived.astype(jnp.float32)
    total = pick(blocks, at).astype(jnp.float32)
    for by in (1, -1):
        arrived = None
        for step in range(1, extent):
            dest = jnp.clip(at + by * (extent - step), 0, extent - 1)
            load = pick(blocks, dest)
            if arrived is not None:
                load = (load.astype(jnp.float32) + arrived.astype(jnp.float32)).astype(jnp.bfloat16)
            senders = range(step) if by == 1 else range(extent - step, extent)
            arrived = step_along(load, axis, by, sizes, senders)
        total = total + arrived.astype(jnp.float32)
    return total


def picked_sum(parts, index):
    if len(parts) == 1:
        return pick(parts[0], index)
    return sum(pick(part, index).astype(F32) for part in parts).astype(BF)


class Summing:
    def __init__(self, pair, sizes, where):
        self.send, self.keep = pair[:2], pair[2:]
        self.sizes, self.where, self.stage = sizes, where, 0

    def axes(self):
        return (0, 1) if self.stage == 1 else (1, 0)

    def loads(self):
        if self.stage == 0:
            return tuple(self.send)
        if self.stage <= 2:
            if self.sizes[0] != 2 or self.sizes[1] != 2:
                return ()
            near, far = self.axes()
            return (
                picked_sum(self.first, 1 - self.where[near]),
                picked_sum(self.second, 1 - self.where[far]),
            )
        return (self.side(1),)

    def side(self, other):
        index = lax.rem(self.where[3] // 2 ** (self.stage - 3) + other, 2)
        return pick(self.both.reshape(-1, 2, *self.both.shape[1:]), index, axis=1)

    def move(self, loads):
        if self.stage == 0:
            axes = (2, 2)
        elif self.stage <= 2:
            axes = self.axes()
        else:
            axes = (3,)
        result = []
        for load, axis in zip(loads, axes):
            if axis == 3:
                result.append(swap_line(load, 2 ** (self.stage - 3), self.sizes))
            else:
                result.append(swap_along(load, axis, self.sizes))
        return tuple(result)

    def add(self, arrived):
        if self.stage == 0:
            grid = (self.sizes[0], self.sizes[1], self.sizes[3])
            self.first, self.second = (
                tuple(part.reshape(grid + part.shape[1:]) for part in parts)
                for parts in zip(self.keep, arrived)
            )
            self.second = tuple(part.transpose(1, 0, 2, 3, 4) for part in self.second)
        elif self.stage <= 2:
            parts = []
            for i, (part, axis) in enumerate(zip((self.first, self.second), self.axes())):
                if arrived:
                    part = picked_sum(part, self.where[axis]).astype(F32) + arrived[i].astype(F32)
                else:
                    part = sum(one.astype(F32) for one in part).astype(BF)
                    part = scatter_axis(part, axis, self.sizes, self.where)
                parts.append(part.astype(BF))
            self.first, self.second = ((part,) for part in parts)
            if self.stage == 2:
                self.both = jnp.concatenate(parts, axis=1)
        else:
            total = self.side(0).astype(F32) + arrived[0].astype(F32)
            self.both = total.astype(BF)
            self.total = total
        self.stage += 1

    def result(self):
        return (self.total if self.sizes[3] > 1 else self.both.astype(F32))[0]


def after(value, other):
    return lax.optimization_barrier((value, other))[0]


def advance(*sums):
    loads = lax.optimization_barrier(tuple(one.loads() for one in sums))
    moved = tuple(one.move(load) for one, load in zip(sums, loads))
    for one, came in zip(sums, lax.optimization_barrier(moved)):
        one.add(came)


def tied(first, second):
    return lax.optimization_barrier((first, second))


def halo_tokens(tokens, reach):
    pieces = [tokens]
    for _ in range(reach):
        pieces.insert(0, passed_along(pieces[0], "group", 1))
    return jnp.concatenate(pieces, axis=0)


def halo_return(rows, own):
    reach = rows.shape[0] // own - 1
    carried = None
    for slot in range(reach):
        piece = rows[slot * own : (slot + 1) * own]
        if carried is not None:
            piece = (piece.astype(F32) + carried.astype(F32)).astype(BF)
        carried = passed_along(piece, "group", -1)
    return rows[reach * own :].astype(F32) + carried.astype(F32)


def shards(tokens, cotangent, positions, attn_weights, ffn_weights, attn_m, attn_v, ffn_m, ffn_v):
    sizes, where = grid_of()
    core = where[2].astype(jnp.int32).reshape(1)
    attn_own, ffn_own = (attn_weights.shape[0], ffn_weights.shape[0])
    devices = math.prod(sizes)
    own = tokens.shape[0]
    reach = (WINDOW - 1) // own + 1

    ffn_full = lax.all_gather(ffn_weights.astype(BF), ("dp", "group"), axis=0)
    window = halo_tokens(tokens, reach)
    place = positions[:, None]
    before = positions[0] + jnp.arange(-reach * own, 0, dtype=positions.dtype)
    cosine, sine_t = rope_tables(jnp.concatenate([before, positions]))

    block = jnp.pad(attn_weights.astype(BF), ((0, rows_up(attn_own) - attn_own), (0, 0)))
    line = lax.all_gather(block, "group", axis=0)
    here = jnp.stack(where).astype(jnp.int32)
    dims = attn_shapes()[:4]
    parts = unpack(
        functools.partial(unpack_pieces_body, dims, attn_own, sizes),
        dims,
        14,
        attn_own,
        devices,
        gather_pieces(line, sizes),
        (here,),
    )
    attn_parts = parts[:4] + cut_gains(parts[4], (D, HD, HD, D))
    normed_b, queries, keys, query_b, key_b, value_b, attended_b, branch, middle = attention(
        window, place, cosine, sine_t, attn_parts
    )

    ffn_full, middle = tied(ffn_full, middle)
    output, grad_middle, *pair = feed_forward(core, middle, cotangent, ffn_full, sizes)
    ffn_sum = Summing(pair, sizes, where)
    advance(ffn_sum)
    loads, grad_middle = tied(ffn_sum.loads(), grad_middle)
    moved = ffn_sum.move(loads)
    kept = (queries, keys, query_b, key_b, value_b)
    (
        grad_branch_b, grad_q_b, grad_k_b, grad_v_b, grad_normed, sum_in, sum_q, sum_k, sum_mid,
    ) = attention_back(grad_middle, branch, window, place, cosine, sine_t, kept, attn_parts)
    pair = pack_grads(
        attn_shapes()[:4],
        [normed_b, normed_b, normed_b, attended_b],
        [grad_q_b, grad_k_b, grad_v_b, grad_branch_b],
        [sum_in, sum_q, sum_k, sum_mid],
        attn_own,
        sizes,
        core,
    )
    ffn_sum.add(after(moved, pair))
    attn_sum = Summing(pair, sizes, where)
    last = 3 + (sizes[3] - 1).bit_length()
    while attn_sum.stage < last:
        moved = ffn_sum.move(ffn_sum.loads()) if ffn_sum.stage < last else None
        if attn_sum.stage == 0:
            attn_sum.add(attn_sum.move(attn_sum.loads()))
        loads = attn_sum.loads()
        if moved is not None:
            ffn_sum.add(after(moved, loads))
        attn_sum.add(attn_sum.move(loads))
    while ffn_sum.stage < last:
        ffn_sum.add(ffn_sum.move(ffn_sum.loads()))
    ffn_grad = ffn_sum.result()[:ffn_own]
    attn_grad = attn_sum.result()[:attn_own]

    grad_kv = halo_return(
        jnp.concatenate([grad_k_b, grad_v_b], axis=1), own
    ).astype(BF)
    w_k, w_v, g_in = attn_parts[1], attn_parts[2], attn_parts[4]
    grad_normed = (
        grad_normed + times_trans(grad_kv[:, :HD], w_k) + times_trans(grad_kv[:, HD:], w_v)
    )
    values = tokens.astype(F32)
    grad_tokens = grad_middle + norm_grad(values, row_norm(values), g_in, grad_normed)[0]
    attn_new, attn_m_new, attn_v_new = adam_step(attn_weights, attn_grad, attn_m, attn_v)
    ffn_new, ffn_m_new, ffn_v_new = adam_step(ffn_weights, ffn_grad, ffn_m, ffn_v)
    return (
        output,
        grad_tokens,
        attn_grad,
        ffn_grad,
        attn_new,
        ffn_new,
        attn_m_new,
        attn_v_new,
        ffn_m_new,
        ffn_v_new,
    )


def solution(mesh):
    placed = (
        P(("dp", "group"), None),
        P(("dp", "group"), None),
        P(("dp", "group")),
        P(("dp", "group"), None),
        P(("dp", "group"), None),
        P(("dp", "group"), None),
        P(("dp", "group"), None),
        P(("dp", "group"), None),
        P(("dp", "group"), None),
    )

    return jax.shard_map(
        shards,
        mesh=mesh,
        in_specs=placed,
        out_specs=(
            P(("dp", "group"), None),
            P(("dp", "group"), None),
            P(("dp", "group"), None),
            P(("dp", "group"), None),
            P(("dp", "group"), None),
            P(("dp", "group"), None),
            P(("dp", "group"), None),
            P(("dp", "group"), None),
            P(("dp", "group"), None),
            P(("dp", "group"), None),
        ),
        check_vma=False,
    )
```

profile of v0, /device:TPU:1, one launch (start us, length us, event | category | flops | bytes accessed | tf_op | source)
XLA Modules:
  0.0 250.9 jit_solution(886443951082149007)
XLA Ops:
  7.2 1.8 convert_bitcast_fusion
  10.0 14.1 %all-gather.1 = bf16[1664,128]{1,0:T(8,128)(2,1)S(1)} all-gather(bf16[416,128]{1,0:T(8,128)(2,1)S(1)} %pad.4), channel_id=3, replica_groups=mesh['dp'=8,'group'=4] {'group'}, dimensions={0}, use_global_device_ids=true | all-gather | bytes 532480 | tf_op jit(solution)/shard_map/all_gather | solution.py:685
  24.2 1.3 collective-permute-start.5
  25.5 1.2 collective-permute-start.2
  26.7 2.3 collective-permute-done.5
  29.0 1.3 collective-permute-start.6
  30.7 1.0 collective-permute-start.3
  31.7 2.2 collective-permute-start
  35.0 5.8 %collective-permute-done.6 = bf16[2,4,208,128]{3,2,1,0:T(8,128)(2,1)S(1)} collective-permute-done((bf16[2,4,208,128]{3,2,1,0:T(8,128)(2,1)S(1)}, bf16[2,4,208,128]{3,2,1,0:T(8,128)(2,1)S(1)}, u32[]{:S(2)}, u32[]{:S(2)}) %collective-permute-start.6) | collective-permute-done | bytes 426016 | tf_op jit(solution)/shard_map/ppermute | solution.py:506
  41.0 4.0 %collective-permute-start.7 = (bf16[16,208,128]{2,1,0:T(8,128)(2,1)S(1)}, bf16[16,208,128]{2,1,0:T(8,128)(2,1)S(1)}, u32[]{:S(2)}, u32[]{:S(2)}) collective-permute-start(bf16[16,208,128]{2,1,0:T(8,128)(2,1)S(1)} %bitcast.131), channel_id=1, source_target_pairs={{0,4},{4,0},{8,12},{12,8},{16,20},{20,16},{24,28},{28,24},{1,5},{5... | collective-permute-start | bytes 2555912 | tf_op jit(solution)/shard_map/ppermute | solution.py:506
  45.1 1.8 collective-permute-start.4
  47.7 5.5 %collective-permute-start.1 = (bf16[256,640]{1,0:T(8,128)(2,1)S(1)}, bf16[256,640]{1,0:T(8,128)(2,1)S(1)}, u32[]{:S(2)}, u32[]{:S(2)}) collective-permute-start(bf16[256,640]{1,0:T(8,128)(2,1)S(1)} %collective-permute-done), channel_id=1, source_target_pairs={{0,1},{1,2},{2,3},{4,5},{5,6},{6,7},{8,9},{9,10},{10,11},{12,13},{... | collective-permute-start | bytes 983048 | tf_op jit(solution)/shard_map/ppermute | solution.py:33
  53.8 2.5 multiply_sine_fusion
  56.3 2.8 %collective-permute-done.1 = bf16[256,640]{1,0:T(8,128)(2,1)S(1)} collective-permute-done((bf16[256,640]{1,0:T(8,128)(2,1)S(1)}, bf16[256,640]{1,0:T(8,128)(2,1)S(1)}, u32[]{:S(2)}, u32[]{:S(2)}) %collective-permute-start.1) | collective-permute-done | bytes 327712 | tf_op jit(solution)/shard_map/ppermute | solution.py:33
  59.2 1.0 copy-done.19
  61.1 5.3 %shard_map.168 = (bf16[640,1024]{1,0:T(8,128)(2,1)}, bf16[640,256]{1,0:T(8,128)(2,1)}, bf16[640,256]{1,0:T(8,128)(2,1)}, bf16[1024,640]{1,0:T(8,128)(2,1)}, f32[16,128]{1,0:T(8,128)}) custom-call(s32[4]{0:T(128)} %pad_add_fusion.at_ref, bf16[16,208,128]{2,1,0:T(8,128)(2,1)} %bitcast.134, bf16[16,208,128]{2,1,0:T(8,128)(2,1)} %collective-permute-done.4.refs_1_, ...), custom_call_target="tpu_custom_call" | custom-call | bytes 6569984 | tf_op jit(solution)/shard_map/pallas_call | solution.py:211
  66.4 1.4 fusion.37
  69.1 9.6 %shard_map.169 = (bf16[768,640]{1,0:T(8,128)(2,1)}, f32[256,1024]{1,0:T(8,128)}, f32[768,256]{1,0:T(8,128)}, bf16[256,1024]{1,0:T(8,128)(2,1)}, bf16[768,256]{1,...) custom-call(bf16[768,640]{1,0:T(8,128)(2,1)} %copy-done.19, ...), custom_call_target="tpu_custom_call" | custom-call | flops 1979711488 | bytes 11018240 | tf_op jit(solution)/shard_map/pallas_call | solution.py:344
  78.7 13.1 %all-gather.5.cloned.1.call-done.blocks = bf16[32,961,128]{2,1,0:T(8,128)(2,1)} async-done(((bf16[1,961,128]{2,1,0:T(8,128)(2,1)}), bf16[32,961,128]{2,1,0:T(8,128)(2,1)}) %all-gather.5.cloned.1.call-update) | async-done | bytes 7872528 | tf_op jit(solution)/shard_map/all_gather | solution.py:678
  91.8 32.2 %shard_map.170 = (bf16[256,640]{1,0:T(8,128)(2,1)}, f32[256,640]{1,0:T(8,128)}, bf16[16,480,128]{2,1,0:T(8,128)(2,1)}, bf16[16,496,128]{2,1,0:T(8,128)(2,1)}, bf...) custom-call(s32[1]{0:T(128)} %bitcast.core_ref, f32[256,640]{1,0:T(8,128)} %get-tuple-element.64.middle, ...), custom_call_target="tpu_custom_call" | custom-call | flops 6039797760 | bytes 15745024 | tf_op jit(solution)/shard_map/pallas_call | solution.py:455
  124.6 6.7 %collective-permute-done.8 = bf16[16,480,128]{2,1,0:T(8,128)(2,1)} collective-permute-done((bf16[16,480,128]{2,1,0:T(8,128)(2,1)}, bf16[16,480,128]{2,1,0:T(8,128)(2,1)}, u32[]{:S(2)}, u32[]{:S(2)}) %collective-permute-start.8) | collective-permute-done | bytes 1966112 | tf_op jit(solution)/shard_map/ppermute | solution.py:506
  131.3 2.4 fusion.2
  133.8 2.4 fusion.6
  136.2 12.0 %shard_map.171 = (bf16[256,640]{1,0:T(8,128)(2,1)}, bf16[256,1024]{1,0:T(8,128)(2,1)}, bf16[768,256]{1,0:T(8,128)(2,1)}, bf16[768,256]{1,0:T(8,128)(2,1)}, f32[2...) custom-call(f32[256,640]{1,0:T(8,128)} %get-tuple-element.76.grad_middle, ...), custom_call_target="tpu_custom_call" | custom-call | flops 3187671040 | bytes 11811840 | tf_op jit(solution)/shard_map/pallas_call | solution.py:344
  148.2 1.0 constant_dynamic-update-slice_fusion.4
  149.2 1.0 constant_dynamic-update-slice_fusion.3
  150.3 1.3 collective-permute-start.10
  151.6 8.2 %collective-permute-done.10 = bf16[256,512]{1,0:T(8,128)(2,1)S(1)} collective-permute-done((bf16[256,512]{1,0:T(8,128)(2,1)S(1)}, bf16[256,512]{1,0:T(8,128)(2,1)S(1)}, u32[]{:S(2)}, u32[]{:S(2)}) %collective-permute-start.10) | collective-permute-done | bytes 262176 | tf_op jit(solution)/shard_map/ppermute | solution.py:33
  160.6 1.3 collective-permute-start.11
  161.9 1.0 collective-permute-start.21
  163.4 10.7 %shard_map.172 = (bf16[16,208,128]{2,1,0:T(8,128)(2,1)}, bf16[16,208,128]{2,1,0:T(8,128)(2,1)}, bf16[16,208,128]{2,1,0:T(8,128)(2,1)}, bf16[16,208,128]{2,1,0:T(8,128)(2,1)}) custom-call(s32[1]{0:T(128)} %bitcast.core_ref, bf16[768,640]{1,0:T(8,128)(2,1)} %get-tuple-element.86.refs_0_.refs_1_.refs_2_, ...), custom_call_target="tpu_custom_call" | custom-call | flops 2516582400 | bytes 3407872 | tf_op jit(solution)/shard_map/pallas_call | solution.py:148
  174.1 1.7 collective-permute-start.12
  176.8 1.3 collective-permute-done.12
  178.2 1.0 collective-permute-start.13
  179.4 1.3 collective-permute-start.16
  180.7 4.5 %collective-permute-done.20 = bf16[2,4,480,128]{3,2,1,0:T(8,128)(2,1)} collective-permute-done((bf16[2,4,480,128]{3,2,1,0:T(8,128)(2,1)}, bf16[2,4,480,128]{3,2,1,0:T(8,128)(2,1)}, u32[]{:S(2)}, u32[]{:S(2)}) %collective-permute-start.20) | collective-permute-done | bytes 983072 | tf_op jit(solution)/shard_map/ppermute | solution.py:506
  185.2 1.6 fusion
  186.9 1.2 collective-permute-start.23
  188.1 1.9 fusion.1
  190.6 3.6 %collective-permute-done.13 = bf16[2,4,208,128]{3,2,1,0:T(8,128)(2,1)S(1)} collective-permute-done((bf16[2,4,208,128]{3,2,1,0:T(8,128)(2,1)S(1)}, bf16[2,4,208,128]{3,2,1,0:T(8,128)(2,1)S(1)}, u32[]{:S(2)}, u32[]{:S(2)}) %collective-permute-start.13) | collective-permute-done | bytes 426016 | tf_op jit(solution)/shard_map/ppermute | solution.py:506
  195.2 1.2 collective-permute-start.17
  196.4 12.9 %collective-permute-done.14 = bf16[4,208,128]{2,1,0:T(8,128)(2,1)S(1)} collective-permute-done((bf16[4,208,128]{2,1,0:T(8,128)(2,1)S(1)}, bf16[4,208,128]{2,1,0:T(8,128)(2,1)S(1)}, u32[]{:S(2)}, u32[]{:S(2)}) %collective-permute-start.14) | collective-permute-done | bytes 213024 | tf_op jit(solution)/shard_map/ppermute | solution.py:506
  209.8 1.9 collective-permute-start.18
  212.9 1.1 fusion.16
  215.0 2.5 collective-permute-start.19
  217.5 10.3 %collective-permute-done.24 = bf16[2,976,128]{2,1,0:T(8,128)(2,1)S(1)} collective-permute-done((bf16[2,976,128]{2,1,0:T(8,128)(2,1)S(1)}, bf16[2,976,128]{2,1,0:T(8,128)(2,1)S(1)}, u32[]{:S(2)}, u32[]{:S(2)}) %collective-permute-start.24) | collective-permute-done | bytes 499744 | tf_op jit(solution)/shard_map/ppermute | solution.py:533
  229.0 13.7 %collective-permute-done.25 = bf16[1,976,128]{2,1,0:T(8,128)(2,1)S(1)} collective-permute-done((bf16[1,976,128]{2,1,0:T(8,128)(2,1)S(1)}, bf16[1,976,128]{2,1,0:T(8,128)(2,1)S(1)}, u32[]{:S(2)}, u32[]{:S(2)}) %collective-permute-start.25) | collective-permute-done | bytes 249888 | tf_op jit(solution)/shard_map/ppermute | solution.py:533
  242.7 1.4 multiply_subtract_fusion
  (112 shorter events, 15.0 us)
Async XLA Ops:
  7.2 84.7 %all-gather.5.cloned.1.call-start = ((), (), s32[]{:S(2)}) async-start(), calls=%async_computation | async-start | bytes 8177664 | tf_op jit(solution)/shard_map/all_gather | solution.py:678
  24.1 7.6 %copy-start.2 = (bf16[256,640]{1,0:T(8,128)(2,1)S(1)}, bf16[256,640]{1,0:T(8,128)(2,1)}, u32[]{:S(2)}) copy-start(bf16[256,640]{1,0:T(8,128)(2,1)} %param.9) | copy-start | bytes 983044
  24.1 9.8 %copy-start.20 = (s32[256]{0:T(256)S(1)}, s32[256]{0:T(256)}, u32[]{:S(2)}) copy-start(s32[256]{0:T(256)} %param.11) | copy-start | bytes 3076
  24.2 4.8 %collective-permute-start.5 = (bf16[4,208,128]{2,1,0:T(8,128)(2,1)S(1)}, bf16[4,208,128]{2,1,0:T(8,128)(2,1)S(1)}, u32[]{:S(2)}, u32[]{:S(2)}) collective-permute-start(bf16[4,208,128]{2,1,0:T(8,128)(2,1)S(1)} %get-tuple-element.120), channel_id=1, source_target_pairs={{0,16},{4,20},{8,24},{12,28},{16,0},{20,4},{24,8},{28,12},{1,17},{... | collective-permute-start | bytes 638984 | tf_op jit(solution)/shard_map/ppermute | solution.py:506
  25.5 5.1 %collective-permute-start.2 = (bf16[4,208,128]{2,1,0:T(8,128)(2,1)S(1)}, bf16[4,208,128]{2,1,0:T(8,128)(2,1)S(1)}, u32[]{:S(2)}, u32[]{:S(2)}) collective-permute-start(bf16[4,208,128]{2,1,0:T(8,128)(2,1)S(1)} %get-tuple-element.121), channel_id=1, source_target_pairs={{0,8},{4,12},{8,0},{12,4},{16,24},{20,28},{24,16},{28,20},{1,9},{5... | collective-permute-start | bytes 638984 | tf_op jit(solution)/shard_map/ppermute | solution.py:506
  29.0 11.8 %collective-permute-start.6 = (bf16[2,4,208,128]{3,2,1,0:T(8,128)(2,1)S(1)}, bf16[2,4,208,128]{3,2,1,0:T(8,128)(2,1)S(1)}, u32[]{:S(2)}, u32[]{:S(2)}) collective-permute-start(bf16[2,4,208,128]{3,2,1,0:T(8,128)(2,1)S(1)} %get-tuple-element.117), channel_id=1, source_target_pairs={{0,8},{4,12},{8,0},{12,4},{16,24},{20,28},{24,16},{28,20},{1,9},{5... | collective-permute-start | bytes 1277960 | tf_op jit(solution)/shard_map/ppermute | solution.py:506
  30.7 14.3 %collective-permute-start.3 = (bf16[2,4,208,128]{3,2,1,0:T(8,128)(2,1)S(1)}, bf16[2,4,208,128]{3,2,1,0:T(8,128)(2,1)S(1)}, u32[]{:S(2)}, u32[]{:S(2)}) collective-permute-start(bf16[2,4,208,128]{3,2,1,0:T(8,128)(2,1)S(1)} %get-tuple-element.123), channel_id=1, source_target_pairs={{0,16},{4,20},{8,24},{12,28},{16,0},{20,4},{24,8},{28,12},{1,17},{... | collective-permute-start | bytes 1277960 | tf_op jit(solution)/shard_map/ppermute | solution.py:506
  31.7 16.0 %collective-permute-start = (bf16[256,640]{1,0:T(8,128)(2,1)S(1)}, bf16[256,640]{1,0:T(8,128)(2,1)S(1)}, u32[]{:S(2)}, u32[]{:S(2)}) collective-permute-start(bf16[256,640]{1,0:T(8,128)(2,1)S(1)} %copy-done.2), channel_id=1, source_target_pairs={{0,1},{1,2},{2,3},{4,5},{5,6},{6,7},{8,9},{9,10},{10,11},{12,13},{... | collective-permute-start | bytes 983048 | tf_op jit(solution)/shard_map/ppermute | solution.py:33
  40.9 18.2 %copy-start = (bf16[2,2,4,208,128]{4,3,2,1,0:T(8,128)(2,1)}, bf16[2,2,4,208,128]{4,3,2,1,0:T(8,128)(2,1)S(1)}, u32[]{:S(2)}) copy-start(bf16[2,2,4,208,128]{4,3,2,1,0:T(8,128)(2,1)S(1)} %pad_maximum_fusion.2) | copy-start | bytes 2555908
  41.0 18.3 %collective-permute-start.7 = (bf16[16,208,128]{2,1,0:T(8,128)(2,1)S(1)}, bf16[16,208,128]{2,1,0:T(8,128)(2,1)S(1)}, u32[]{:S(2)}, u32[]{:S(2)}) collective-permute-start(bf16[16,208,128]{2,1,0:T(8,128)(2,1)S(1)} %bitcast.131), channel_id=1, source_target_pairs={{0,4},{4,0},{8,12},{12,8},{16,20},{20,16},{24,28},{28,24},{1,5},{5... | collective-permute-start | bytes 2555912 | tf_op jit(solution)/shard_map/ppermute | solution.py:506
  45.1 15.1 %copy-start.1 = (bf16[2,2,4,208,128]{4,3,2,1,0:T(8,128)(2,1)}, bf16[2,2,4,208,128]{4,3,2,1,0:T(8,128)(2,1)S(1)}, u32[]{:S(2)}) copy-start(bf16[2,2,4,208,128]{4,3,2,1,0:T(8,128)(2,1)S(1)} %pad_maximum_fusion.1) | copy-start | bytes 2555908
  45.1 15.1 %collective-permute-start.4 = (bf16[16,208,128]{2,1,0:T(8,128)(2,1)S(1)}, bf16[16,208,128]{2,1,0:T(8,128)(2,1)}, u32[]{:S(2)}, u32[]{:S(2)}) collective-permute-start(bf16[16,208,128]{2,1,0:T(8,128)(2,1)S(1)} %bitcast.133), channel_id=1, source_target_pairs={{0,4},{4,0},{8,12},{12,8},{16,20},{20,16},{24,28},{28,24},{1,5},{5... | collective-permute-start | bytes 2555912 | tf_op jit(solution)/shard_map/ppermute | solution.py:506
  47.7 11.4 %collective-permute-start.1 = (bf16[256,640]{1,0:T(8,128)(2,1)S(1)}, bf16[256,640]{1,0:T(8,128)(2,1)S(1)}, u32[]{:S(2)}, u32[]{:S(2)}) collective-permute-start(bf16[256,640]{1,0:T(8,128)(2,1)S(1)} %collective-permute-done), channel_id=1, source_target_pairs={{0,1},{1,2},{2,3},{4,5},{5,6},{6,7},{8,9},{9,10},{10,11},{12,13},{... | collective-permute-start | bytes 983048 | tf_op jit(solution)/shard_map/ppermute | solution.py:33
  59.2 1.0 copy-start.19
  60.2 0.9 copy-start.7
  124.1 7.2 %collective-permute-start.9 = (bf16[16,496,128]{2,1,0:T(8,128)(2,1)}, bf16[16,496,128]{2,1,0:T(8,128)(2,1)S(1)}, u32[]{:S(2)}, u32[]{:S(2)}) collective-permute-start(bf16[16,496,128]{2,1,0:T(8,128)(2,1)} %get-tuple-element.71), channel_id=1, source_target_pairs={{0,4},{4,0},{8,12},{12,8},{16,20},{20,16},{24,28},{28,24},{1,5},{5... | collective-permute-start | bytes 6094856 | tf_op jit(solution)/shard_map/ppermute | solution.py:506
  124.3 7.0 %collective-permute-start.8 = (bf16[16,480,128]{2,1,0:T(8,128)(2,1)}, bf16[16,480,128]{2,1,0:T(8,128)(2,1)}, u32[]{:S(2)}, u32[]{:S(2)}) collective-permute-start(bf16[16,480,128]{2,1,0:T(8,128)(2,1)} %get-tuple-element.70), channel_id=1, source_target_pairs={{0,4},{4,0},{8,12},{12,8},{16,20},{20,16},{24,28},{28,24},{1,5},{5... | collective-permute-start | bytes 5898248 | tf_op jit(solution)/shard_map/ppermute | solution.py:506
  124.6 9.2 %copy-start.5 = (bf16[16,480,128]{2,1,0:T(8,128)(2,1)S(1)}, bf16[16,480,128]{2,1,0:T(8,128)(2,1)}, u32[]{:S(2)}) copy-start(bf16[16,480,128]{2,1,0:T(8,128)(2,1)} %get-tuple-element.67) | copy-start | bytes 5898244
  150.3 9.5 %collective-permute-start.10 = (bf16[256,512]{1,0:T(8,128)(2,1)S(1)}, bf16[256,512]{1,0:T(8,128)(2,1)S(1)}, u32[]{:S(2)}, u32[]{:S(2)}) collective-permute-start(bf16[256,512]{1,0:T(8,128)(2,1)S(1)} %slice.72), channel_id=1, source_target_pairs={{1,0},{2,1},{3,2},{5,4},{6,5},{7,6},{9,8},{10,9},{11,10},{13,12},{... | collective-permute-start | bytes 786440 | tf_op jit(solution)/shard_map/ppermute | solution.py:33
  160.6 15.4 %collective-permute-start.11 = (bf16[256,512]{1,0:T(8,128)(2,1)}, bf16[256,512]{1,0:T(8,128)(2,1)S(1)}, u32[]{:S(2)}, u32[]{:S(2)}) collective-permute-start(bf16[256,512]{1,0:T(8,128)(2,1)} %add_convert_fusion.9), channel_id=1, source_target_pairs={{1,0},{2,1},{3,2},{5,4},{6,5},{7,6},{9,8},{10,9},{11,10},{13,12},{... | collective-permute-start | bytes 786440 | tf_op jit(solution)/shard_map/ppermute | solution.py:33
  161.9 23.3 %collective-permute-start.21 = (bf16[2,4,496,128]{3,2,1,0:T(8,128)(2,1)}, bf16[2,4,496,128]{3,2,1,0:T(8,128)(2,1)}, u32[]{:S(2)}, u32[]{:S(2)}) collective-permute-start(bf16[2,4,496,128]{3,2,1,0:T(8,128)(2,1)} %fusion.2), channel_id=1, source_target_pairs={{0,8},{4,12},{8,0},{12,4},{16,24},{20,28},{24,16},{28,20},{1,9},{5... | collective-permute-start | bytes 3047432 | tf_op jit(solution)/shard_map/ppermute | solution.py:506
  162.9 22.2 %collective-permute-start.20 = (bf16[2,4,480,128]{3,2,1,0:T(8,128)(2,1)}, bf16[2,4,480,128]{3,2,1,0:T(8,128)(2,1)}, u32[]{:S(2)}, u32[]{:S(2)}) collective-permute-start(bf16[2,4,480,128]{3,2,1,0:T(8,128)(2,1)} %fusion.6), channel_id=1, source_target_pairs={{0,16},{4,20},{8,24},{12,28},{16,0},{20,4},{24,8},{28,12},{1,17},{... | collective-permute-start | bytes 2949128 | tf_op jit(solution)/shard_map/ppermute | solution.py:506
  163.4 12.6 %copy-start.16 = (bf16[640,256]{1,0:T(8,128)(2,1)S(1)}, bf16[640,256]{1,0:T(8,128)(2,1)}, u32[]{:S(2)}) copy-start(bf16[640,256]{1,0:T(8,128)(2,1)} %get-tuple-element.59.w_k) | copy-start | bytes 983044
  174.1 2.2 copy-start.12
  174.1 2.2 copy-start.15
  174.1 4.0 %collective-permute-start.12 = (bf16[16,208,128]{2,1,0:T(8,128)(2,1)}, bf16[16,208,128]{2,1,0:T(8,128)(2,1)S(1)}, u32[]{:S(2)}, u32[]{:S(2)}) collective-permute-start(bf16[16,208,128]{2,1,0:T(8,128)(2,1)} %get-tuple-element.95), channel_id=1, source_target_pairs={{0,4},{4,0},{8,12},{12,8},{16,20},{20,16},{24,28},{28,24},{1,5},{5... | collective-permute-start | bytes 2555912 | tf_op jit(solution)/shard_map/ppermute | solution.py:506
  175.9 3.4 %collective-permute-start.15 = (bf16[16,208,128]{2,1,0:T(8,128)(2,1)}, bf16[16,208,128]{2,1,0:T(8,128)(2,1)S(1)}, u32[]{:S(2)}, u32[]{:S(2)}) collective-permute-start(bf16[16,208,128]{2,1,0:T(8,128)(2,1)} %get-tuple-element.97), channel_id=1, source_target_pairs={{0,4},{4,0},{8,12},{12,8},{16,20},{20,16},{24,28},{28,24},{1,5},{5... | collective-permute-start | bytes 2555912 | tf_op jit(solution)/shard_map/ppermute | solution.py:506
  176.0 2.1 copy-start.9
  176.4 2.9 %copy-start.8 = (bf16[16,208,128]{2,1,0:T(8,128)(2,1)S(1)}, bf16[16,208,128]{2,1,0:T(8,128)(2,1)}, u32[]{:S(2)}) copy-start(bf16[16,208,128]{2,1,0:T(8,128)(2,1)} %get-tuple-element.96) | copy-start | bytes 2555908
  176.4 8.9 %copy-start.3 = (bf16[16,496,128]{2,1,0:T(8,128)(2,1)S(1)}, bf16[16,496,128]{2,1,0:T(8,128)(2,1)}, u32[]{:S(2)}) copy-start(bf16[16,496,128]{2,1,0:T(8,128)(2,1)} %get-tuple-element.73) | copy-start | bytes 6094852
  178.2 16.0 %collective-permute-start.13 = (bf16[2,4,208,128]{3,2,1,0:T(8,128)(2,1)S(1)}, bf16[2,4,208,128]{3,2,1,0:T(8,128)(2,1)S(1)}, u32[]{:S(2)}, u32[]{:S(2)}) collective-permute-start(bf16[2,4,208,128]{3,2,1,0:T(8,128)(2,1)S(1)} %fusion.20), channel_id=1, source_target_pairs={{0,16},{4,20},{8,24},{12,28},{16,0},{20,4},{24,8},{28,12},{1,17},{... | collective-permute-start | bytes 1277960 | tf_op jit(solution)/shard_map/ppermute | solution.py:506
  179.4 8.7 %copy-start.6 = (bf16[16,480,128]{2,1,0:T(8,128)(2,1)S(1)}, bf16[16,480,128]{2,1,0:T(8,128)(2,1)}, u32[]{:S(2)}) copy-start(bf16[16,480,128]{2,1,0:T(8,128)(2,1)} %get-tuple-element.67) | copy-start | bytes 5898244
  179.4 15.6 %collective-permute-start.16 = (bf16[2,4,208,128]{3,2,1,0:T(8,128)(2,1)S(1)}, bf16[2,4,208,128]{3,2,1,0:T(8,128)(2,1)S(1)}, u32[]{:S(2)}, u32[]{:S(2)}) collective-permute-start(bf16[2,4,208,128]{3,2,1,0:T(8,128)(2,1)S(1)} %fusion.22), channel_id=1, source_target_pairs={{0,8},{4,12},{8,0},{12,4},{16,24},{20,28},{24,16},{28,20},{1,9},{5... | collective-permute-start | bytes 1277960 | tf_op jit(solution)/shard_map/ppermute | solution.py:506
  186.9 24.7 %collective-permute-start.23 = (bf16[4,496,128]{2,1,0:T(8,128)(2,1)S(1)}, bf16[4,496,128]{2,1,0:T(8,128)(2,1)S(1)}, u32[]{:S(2)}, u32[]{:S(2)}) collective-permute-start(bf16[4,496,128]{2,1,0:T(8,128)(2,1)S(1)} %dynamic-slice_bitcast_fusion), channel_id=1, source_target_pairs={{0,16},{4,20},{8,24},{12,28},{16,0},{20,4},{24,8},{28,12},{1,17},{... | collective-permute-start | bytes 1523720 | tf_op jit(solution)/shard_map/ppermute | solution.py:506
  190.1 21.6 %collective-permute-start.22 = (bf16[4,480,128]{2,1,0:T(8,128)(2,1)S(1)}, bf16[4,480,128]{2,1,0:T(8,128)(2,1)S(1)}, u32[]{:S(2)}, u32[]{:S(2)}) collective-permute-start(bf16[4,480,128]{2,1,0:T(8,128)(2,1)S(1)} %dynamic-slice_bitcast_fusion.2), channel_id=1, source_target_pairs={{0,8},{4,12},{8,0},{12,4},{16,24},{20,28},{24,16},{28,20},{1,9},{5... | collective-permute-start | bytes 1474568 | tf_op jit(solution)/shard_map/ppermute | solution.py:506
  194.4 14.9 %collective-permute-start.14 = (bf16[4,208,128]{2,1,0:T(8,128)(2,1)S(1)}, bf16[4,208,128]{2,1,0:T(8,128)(2,1)S(1)}, u32[]{:S(2)}, u32[]{:S(2)}) collective-permute-start(bf16[4,208,128]{2,1,0:T(8,128)(2,1)S(1)} %dynamic-slice_bitcast_fusion.5), channel_id=1, source_target_pairs={{0,8},{4,12},{8,0},{12,4},{16,24},{20,28},{24,16},{28,20},{1,9},{5... | collective-permute-start | bytes 638984 | tf_op jit(solution)/shard_map/ppermute | solution.py:506
  195.2 14.4 %collective-permute-start.17 = (bf16[4,208,128]{2,1,0:T(8,128)(2,1)S(1)}, bf16[4,208,128]{2,1,0:T(8,128)(2,1)S(1)}, u32[]{:S(2)}, u32[]{:S(2)}) collective-permute-start(bf16[4,208,128]{2,1,0:T(8,128)(2,1)S(1)} %dynamic-slice_bitcast_fusion.4), channel_id=1, source_target_pairs={{0,16},{4,20},{8,24},{12,28},{16,0},{20,4},{24,8},{28,12},{1,17},{... | collective-permute-start | bytes 638984 | tf_op jit(solution)/shard_map/ppermute | solution.py:506
  209.8 5.1 %collective-permute-start.18 = (bf16[2,416,128]{2,1,0:T(8,128)(2,1)S(1)}, bf16[2,416,128]{2,1,0:T(8,128)(2,1)S(1)}, u32[]{:S(2)}, u32[]{:S(2)}) collective-permute-start(bf16[2,416,128]{2,1,0:T(8,128)(2,1)S(1)} %dynamic-slice_bitcast_fusion.3), channel_id=1, source_target_pairs={{0,1},{1,0},{2,3},{3,2},{4,5},{5,4},{6,7},{7,6},{8,9},{9,8},{10,11... | collective-permute-start | bytes 638984 | tf_op jit(solution)/shard_map/ppermute | solution.py:533
  211.8 1.1 copy-start.11
  212.1 15.7 %collective-permute-start.24 = (bf16[2,976,128]{2,1,0:T(8,128)(2,1)S(1)}, bf16[2,976,128]{2,1,0:T(8,128)(2,1)S(1)}, u32[]{:S(2)}, u32[]{:S(2)}) collective-permute-start(bf16[2,976,128]{2,1,0:T(8,128)(2,1)S(1)} %dynamic-slice_bitcast_fusion.1), channel_id=1, source_target_pairs={{0,1},{1,0},{2,3},{3,2},{4,5},{5,4},{6,7},{7,6},{8,9},{9,8},{10,11... | collective-permute-start | bytes 1499144 | tf_op jit(solution)/shard_map/ppermute | solution.py:533
  214.0 14.0 %copy-start.10 = (f32[401,128]{1,0:T(8,128)S(1)}, f32[401,128]{1,0:T(8,128)}, u32[]{:S(2)}) copy-start(f32[401,128]{1,0:T(8,128)} %param.12) | copy-start | bytes 615940
  214.0 14.0 %copy-start.17 = (f32[401,128]{1,0:T(8,128)S(1)}, f32[401,128]{1,0:T(8,128)}, u32[]{:S(2)}) copy-start(f32[401,128]{1,0:T(8,128)} %param.14) | copy-start | bytes 615940
  214.0 14.0 %copy-start.18 = (f32[401,128]{1,0:T(8,128)S(1)}, f32[401,128]{1,0:T(8,128)}, u32[]{:S(2)}) copy-start(f32[401,128]{1,0:T(8,128)} %param.15) | copy-start | bytes 615940
  214.9 27.7 %copy-start.4 = (f32[961,128]{1,0:T(8,128)S(1)}, f32[961,128]{1,0:T(8,128)}, u32[]{:S(2)}) copy-start(f32[961,128]{1,0:T(8,128)} %param.13) | copy-start | bytes 1476100
  214.9 27.7 %copy-start.13 = (f32[961,128]{1,0:T(8,128)S(1)}, f32[961,128]{1,0:T(8,128)}, u32[]{:S(2)}) copy-start(f32[961,128]{1,0:T(8,128)} %param.16) | copy-start | bytes 1476100
  215.0 27.7 %copy-start.14 = (f32[961,128]{1,0:T(8,128)S(1)}, f32[961,128]{1,0:T(8,128)}, u32[]{:S(2)}) copy-start(f32[961,128]{1,0:T(8,128)} %param.17) | copy-start | bytes 1476100
  215.0 13.0 %collective-permute-start.19 = (bf16[1,416,128]{2,1,0:T(8,128)(2,1)S(1)}, bf16[1,416,128]{2,1,0:T(8,128)(2,1)S(1)}, u32[]{:S(2)}, u32[]{:S(2)}) collective-permute-start(bf16[1,416,128]{2,1,0:T(8,128)(2,1)S(1)} %constant_dynamic-slice_fusion), channel_id=1, source_target_pairs={{0,2},{1,3},{2,0},{3,1},{4,6},{5,7},{6,4},{7,5},{8,10},{9,11},{10,... | collective-permute-start | bytes 319496 | tf_op jit(solution)/shard_map/ppermute | solution.py:533
  227.9 14.8 %collective-permute-start.25 = (bf16[1,976,128]{2,1,0:T(8,128)(2,1)S(1)}, bf16[1,976,128]{2,1,0:T(8,128)(2,1)S(1)}, u32[]{:S(2)}, u32[]{:S(2)}) collective-permute-start(bf16[1,976,128]{2,1,0:T(8,128)(2,1)S(1)} %constant_dynamic-slice_fusion.1), channel_id=1, source_target_pairs={{0,2},{1,3},{2,0},{3,1},{4,6},{5,7},{6,4},{7,5},{8,10},{9,11},{10,... | collective-permute-start | bytes 749576 | tf_op jit(solution)/shard_map/ppermute | solution.py:533
Sparse Core Ops, SparseCore 0:
  11.5 80.3 all-gather.4
where the time goes:
time: 252 us; the launch traced here: 251 us
  waiting for transfers between devices  86.7 us (34%)
  Pallas kernels  69.9 us (28%)
  starting transfers between devices  35.1 us (14%)
  other arithmetic  21.3 us (8%)
  between operations  14.6 us (6%)
  blocking collectives  14.1 us (6%)
  local copies, waits for them, and re-layouts  8.47 us (3%)
    ppermute x18, waiting for transfers between devices, swap_along(): return lax.ppermute(value, 'dp', pairs)  37.7 us
    pallas_call x1, Pallas kernels, feed_forward(): pl.pallas_call(functools.partial(feed_forward_body, dims_list, own_rows,...  32.2 us
    ppermute x4, waiting for transfers between devices, swap_line(): return lax.ppermute(value, 'group', [(i, i ^ bit) for i in range(sizes[3])])  24.9 us
    pallas_call x2, Pallas kernels, in_vmem(): pl.pallas_call(body, out_shape=out_shape, in_specs=[vmem] * len(args), ou...  21.7 us
    ppermute x18, starting transfers between devices, swap_along(): return lax.ppermute(value, 'dp', pairs)  20.3 us
    all_gather x1, blocking collectives, shards(): line = lax.all_gather(block, 'group', axis=0)  14.1 us
    all_gather x1, waiting for transfers between devices, shards(): ffn_full = lax.all_gather(ffn_weights.astype(BF), ('dp', 'group'), axis=0)  13.1 us
    ppermute x4, waiting for transfers between devices, passed_along(): return lax.ppermute(shard, axis, pairs)  11 us
  transfers between devices with their start and end apart: 27, of which 17 were waited for; matrix products, arithmetic and copies ran while one was open for 7% of the time, Pallas kernels for 10%

commit v1 on v0

--- a/solution.py
+++ b/solution.py
@@ -573,6 +573,9 @@
         return (0, 1) if self.stage == 1 else (1, 0)
 
     def loads(self):
+        return self.leaving()
+
+    def leaving(self):
         if self.stage == 0:
             return tuple(self.send)
         if self.stage <= 2:
@@ -638,13 +641,6 @@
     return lax.optimization_barrier((value, other))[0]
 
 
-def advance(*sums):
-    loads = lax.optimization_barrier(tuple(one.loads() for one in sums))
-    moved = tuple(one.move(load) for one, load in zip(sums, loads))
-    for one, came in zip(sums, lax.optimization_barrier(moved)):
-        one.add(came)
-
-
 def tied(first, second):
     return lax.optimization_barrier((first, second))
 
@@ -702,9 +698,8 @@
     ffn_full, middle = tied(ffn_full, middle)
     output, grad_middle, *pair = feed_forward(core, middle, cotangent, ffn_full, sizes)
     ffn_sum = Summing(pair, sizes, where)
-    advance(ffn_sum)
-    loads, grad_middle = tied(ffn_sum.loads(), grad_middle)
-    moved = ffn_sum.move(loads)
+    ffn_sum.add(ffn_sum.move(ffn_sum.loads()))
+    moved = ffn_sum.move(ffn_sum.loads())
     kept = (queries, keys, query_b, key_b, value_b)
     (
         grad_branch_b, grad_q_b, grad_k_b, grad_v_b, grad_normed, sum_in, sum_q, sum_k, sum_mid,

time: 252 us -> 255 us (1.012)
  waiting for transfers between devices: 86.7 us -> 90.4 us
  other arithmetic: 21.3 us -> 18.5 us
    ppermute x18, waiting for transfers between devices: 37.7 us -> 46.5 us  [swap_along(): return lax.ppermute(value, 'dp', pairs)]
    ppermute x4, waiting for transfers between devices: 24.9 us -> 20.2 us  [swap_line(): return lax.ppermute(value, 'group', [(i, i ^ bit) for i in range(sizes[3])])]
    ppermute x4, starting transfers between devices: 4.5 us -> 7.97 us  [swap_line(): return lax.ppermute(value, 'group', [(i, i ^ bit) for i in range(sizes[3])])]
  transfers between devices with their start and end apart: 27 -> 27, of which waited for: 17 -> 13; matrix products, arithmetic and copies ran while one was open for 7% -> 9% of each run, Pallas kernels for 10% -> 15%
where the time goes in v1:
time: 255 us; the launch traced here: 253 us
  waiting for transfers between devices  90.4 us (35%)
  Pallas kernels  69.7 us (27%)
  starting transfers between devices  37.6 us (15%)
  other arithmetic  18.5 us (7%)
  between operations  14.6 us (6%)
  blocking collectives  14.1 us (6%)
  local copies, waits for them, and re-layouts  7.75 us (3%)
    ppermute x18, waiting for transfers between devices, swap_along(): return lax.ppermute(value, 'dp', pairs)  46.5 us
    pallas_call x1, Pallas kernels, feed_forward(): pl.pallas_call(functools.partial(feed_forward_body, dims_list, own_rows,...  32.2 us
    pallas_call x2, Pallas kernels, in_vmem(): pl.pallas_call(body, out_shape=out_shape, in_specs=[vmem] * len(args), ou...  21.5 us
    ppermute x4, waiting for transfers between devices, swap_line(): return lax.ppermute(value, 'group', [(i, i ^ bit) for i in range(sizes[3])])  20.2 us
    ppermute x18, starting transfers between devices, swap_along(): return lax.ppermute(value, 'dp', pairs)  19.1 us
    all_gather x1, blocking collectives, shards(): line = lax.all_gather(block, 'group', axis=0)  14.1 us
    all_gather x1, waiting for transfers between devices, shards(): ffn_full = lax.all_gather(ffn_weights.astype(BF), ('dp', 'group'), axis=0)  13.1 us
    pallas_call x1, Pallas kernels, pack_grads(): pl.pallas_call(functools.partial(pack_body, jobs, own, padded, sizes), ou...  10.7 us
  transfers between devices with their start and end apart: 27, of which 13 were waited for; matrix products, arithmetic and copies ran while one was open for 9% of the time, Pallas kernels for 15%

profile of v1, /device:TPU:1, one launch (start us, length us, event | category | flops | bytes accessed | tf_op | source)
XLA Modules:
  0.0 253.3 jit_solution(4461095327494037327)
XLA Ops:
  7.2 1.8 convert_bitcast_fusion
  9.0 0.9 convert_element_type.278
  10.0 14.1 %all-gather.1 = bf16[1664,128]{1,0:T(8,128)(2,1)S(1)} all-gather(bf16[416,128]{1,0:T(8,128)(2,1)S(1)} %pad.4), channel_id=3, replica_groups=mesh['dp'=8,'group'=4] {'group'}, dimensions={0}, use_global_device_ids=true | all-gather | bytes 532480 | tf_op jit(solution)/shard_map/all_gather | solution.py:681
  24.2 1.3 collective-permute-start.5
  25.5 1.2 collective-permute-start.2
  26.7 2.3 collective-permute-done.5
  29.0 1.3 collective-permute-start.6
  30.7 1.0 collective-permute-start.3
  31.7 2.2 collective-permute-start
  35.0 5.8 %collective-permute-done.6 = bf16[2,4,208,128]{3,2,1,0:T(8,128)(2,1)S(1)} collective-permute-done((bf16[2,4,208,128]{3,2,1,0:T(8,128)(2,1)S(1)}, bf16[2,4,208,128]{3,2,1,0:T(8,128)(2,1)S(1)}, u32[]{:S(2)}, u32[]{:S(2)}) %collective-permute-start.6) | collective-permute-done | bytes 426016 | tf_op jit(solution)/shard_map/ppermute | solution.py:506
  41.0 4.0 %collective-permute-start.7 = (bf16[16,208,128]{2,1,0:T(8,128)(2,1)S(1)}, bf16[16,208,128]{2,1,0:T(8,128)(2,1)S(1)}, u32[]{:S(2)}, u32[]{:S(2)}) collective-permute-start(bf16[16,208,128]{2,1,0:T(8,128)(2,1)S(1)} %bitcast.131), channel_id=1, source_target_pairs={{0,4},{4,0},{8,12},{12,8},{16,20},{20,16},{24,28},{28,24},{1,5},{5... | collective-permute-start | bytes 2555912 | tf_op jit(solution)/shard_map/ppermute | solution.py:506
  45.1 1.8 collective-permute-start.4
  47.7 5.5 %collective-permute-start.1 = (bf16[256,640]{1,0:T(8,128)(2,1)S(1)}, bf16[256,640]{1,0:T(8,128)(2,1)S(1)}, u32[]{:S(2)}, u32[]{:S(2)}) collective-permute-start(bf16[256,640]{1,0:T(8,128)(2,1)S(1)} %collective-permute-done), channel_id=1, source_target_pairs={{0,1},{1,2},{2,3},{4,5},{5,6},{6,7},{8,9},{9,10},{10,11},{12,13},{... | collective-permute-start | bytes 983048 | tf_op jit(solution)/shard_map/ppermute | solution.py:33
  53.8 2.5 multiply_sine_fusion
  56.3 2.8 %collective-permute-done.1 = bf16[256,640]{1,0:T(8,128)(2,1)S(1)} collective-permute-done((bf16[256,640]{1,0:T(8,128)(2,1)S(1)}, bf16[256,640]{1,0:T(8,128)(2,1)S(1)}, u32[]{:S(2)}, u32[]{:S(2)}) %collective-permute-start.1) | collective-permute-done | bytes 327712 | tf_op jit(solution)/shard_map/ppermute | solution.py:33
  59.2 1.0 copy-done.18
  61.1 5.3 %shard_map.168 = (bf16[640,1024]{1,0:T(8,128)(2,1)}, bf16[640,256]{1,0:T(8,128)(2,1)}, bf16[640,256]{1,0:T(8,128)(2,1)}, bf16[1024,640]{1,0:T(8,128)(2,1)}, f32[16,128]{1,0:T(8,128)}) custom-call(s32[4]{0:T(128)} %pad_add_fusion.at_ref, bf16[16,208,128]{2,1,0:T(8,128)(2,1)} %bitcast.134, bf16[16,208,128]{2,1,0:T(8,128)(2,1)} %collective-permute-done.4.refs_1_, ...), custom_call_target="tpu_custom_call" | custom-call | bytes 6569984 | tf_op jit(solution)/shard_map/pallas_call | solution.py:211
  66.4 1.4 fusion.37
  69.1 9.6 %shard_map.169 = (bf16[768,640]{1,0:T(8,128)(2,1)}, f32[256,1024]{1,0:T(8,128)}, f32[768,256]{1,0:T(8,128)}, bf16[256,1024]{1,0:T(8,128)(2,1)}, bf16[768,256]{1,...) custom-call(bf16[768,640]{1,0:T(8,128)(2,1)} %copy-done.18, ...), custom_call_target="tpu_custom_call" | custom-call | flops 1979711488 | bytes 11018240 | tf_op jit(solution)/shard_map/pallas_call | solution.py:344
  78.7 13.1 %all-gather.5.cloned.1.call-done.blocks = bf16[32,961,128]{2,1,0:T(8,128)(2,1)} async-done(((bf16[1,961,128]{2,1,0:T(8,128)(2,1)}), bf16[32,961,128]{2,1,0:T(8,128)(2,1)}) %all-gather.5.cloned.1.call-update) | async-done | bytes 7872528 | tf_op jit(solution)/shard_map/all_gather | solution.py:674
  91.8 32.2 %shard_map.170 = (bf16[256,640]{1,0:T(8,128)(2,1)}, f32[256,640]{1,0:T(8,128)}, bf16[16,480,128]{2,1,0:T(8,128)(2,1)}, bf16[16,496,128]{2,1,0:T(8,128)(2,1)}, bf...) custom-call(s32[1]{0:T(128)} %bitcast.core_ref, f32[256,640]{1,0:T(8,128)} %get-tuple-element.57.middle, ...), custom_call_target="tpu_custom_call" | custom-call | flops 6039797760 | bytes 15745024 | tf_op jit(solution)/shard_map/pallas_call | solution.py:455
  124.3 11.8 %shard_map.171 = (bf16[256,640]{1,0:T(8,128)(2,1)}, bf16[256,1024]{1,0:T(8,128)(2,1)}, bf16[768,256]{1,0:T(8,128)(2,1)}, bf16[768,256]{1,0:T(8,128)(2,1)}, f32[2...) custom-call(f32[256,640]{1,0:T(8,128)} %get-tuple-element.60.grad_middle, ...), custom_call_target="tpu_custom_call" | custom-call | flops 3187671040 | bytes 11811840 | tf_op jit(solution)/shard_map/pallas_call | solution.py:344
  136.1 1.0 constant_dynamic-update-slice_fusion.4
  137.2 1.0 constant_dynamic-update-slice_fusion.3
  138.2 1.3 collective-permute-start.8
  139.9 7.9 %collective-permute-done.8 = bf16[256,512]{1,0:T(8,128)(2,1)S(1)} collective-permute-done((bf16[256,512]{1,0:T(8,128)(2,1)S(1)}, bf16[256,512]{1,0:T(8,128)(2,1)S(1)}, u32[]{:S(2)}, u32[]{:S(2)}) %collective-permute-start.8) | collective-permute-done | bytes 262176 | tf_op jit(solution)/shard_map/ppermute | solution.py:33
  147.8 1.5 collective-permute-start.9
  149.3 10.7 %shard_map.172 = (bf16[16,208,128]{2,1,0:T(8,128)(2,1)}, bf16[16,208,128]{2,1,0:T(8,128)(2,1)}, bf16[16,208,128]{2,1,0:T(8,128)(2,1)}, bf16[16,208,128]{2,1,0:T(8,128)(2,1)}) custom-call(s32[1]{0:T(128)} %bitcast.core_ref, bf16[768,640]{1,0:T(8,128)(2,1)} %get-tuple-element.70.refs_0_.refs_1_.refs_2_, ...), custom_call_target="tpu_custom_call" | custom-call | flops 2516582400 | bytes 3407872 | tf_op jit(solution)/shard_map/pallas_call | solution.py:148
  160.0 1.2 collective-permute-start.10
  162.2 1.3 collective-permute-done.10
  163.6 1.3 collective-permute-start.11
  164.9 1.5 fusion.7
  166.9 1.5 fusion.2
  170.1 4.6 %collective-permute-done.11 = bf16[2,4,208,128]{3,2,1,0:T(8,128)(2,1)S(1)} collective-permute-done((bf16[2,4,208,128]{3,2,1,0:T(8,128)(2,1)S(1)}, bf16[2,4,208,128]{3,2,1,0:T(8,128)(2,1)S(1)}, u32[]{:S(2)}, u32[]{:S(2)}) %collective-permute-start.11) | collective-permute-done | bytes 426016 | tf_op jit(solution)/shard_map/ppermute | solution.py:506
  174.8 1.0 collective-permute-start.12
  175.9 24.9 %collective-permute-done.14 = bf16[2,4,208,128]{3,2,1,0:T(8,128)(2,1)S(1)} collective-permute-done((bf16[2,4,208,128]{3,2,1,0:T(8,128)(2,1)S(1)}, bf16[2,4,208,128]{3,2,1,0:T(8,128)(2,1)S(1)}, u32[]{:S(2)}, u32[]{:S(2)}) %collective-permute-start.14) | collective-permute-done | bytes 426016 | tf_op jit(solution)/shard_map/ppermute | solution.py:506
  202.0 1.6 fusion
  204.3 1.6 fusion.1
  206.9 2.4 collective-permute-start.16
  209.3 6.1 %collective-permute-done.22 = bf16[4,480,128]{2,1,0:T(8,128)(2,1)S(1)} collective-permute-done((bf16[4,480,128]{2,1,0:T(8,128)(2,1)S(1)}, bf16[4,480,128]{2,1,0:T(8,128)(2,1)S(1)}, u32[]{:S(2)}, u32[]{:S(2)}) %collective-permute-start.22) | collective-permute-done | bytes 491552 | tf_op jit(solution)/shard_map/ppermute | solution.py:506
  215.4 1.2 collective-permute-done.23
  217.0 2.4 collective-permute-start.24
  219.4 1.1 fusion.16
  220.7 1.7 collective-permute-start.17
  222.3 7.8 %collective-permute-done.24 = bf16[2,976,128]{2,1,0:T(8,128)(2,1)S(1)} collective-permute-done((bf16[2,976,128]{2,1,0:T(8,128)(2,1)S(1)}, bf16[2,976,128]{2,1,0:T(8,128)(2,1)S(1)}, u32[]{:S(2)}, u32[]{:S(2)}) %collective-permute-start.24) | collective-permute-done | bytes 499744 | tf_op jit(solution)/shard_map/ppermute | solution.py:533
  230.3 1.4 collective-permute-start.25
  232.7 12.4 %collective-permute-done.25 = bf16[1,976,128]{2,1,0:T(8,128)(2,1)S(1)} collective-permute-done((bf16[1,976,128]{2,1,0:T(8,128)(2,1)S(1)}, bf16[1,976,128]{2,1,0:T(8,128)(2,1)S(1)}, u32[]{:S(2)}, u32[]{:S(2)}) %collective-permute-start.25) | collective-permute-done | bytes 249888 | tf_op jit(solution)/shard_map/ppermute | solution.py:533
  245.1 1.4 multiply_subtract_fusion
  (110 shorter events, 14.1 us)
Async XLA Ops:
  7.2 84.7 %all-gather.5.cloned.1.call-start = ((), (), s32[]{:S(2)}) async-start(), calls=%async_computation | async-start | bytes 8177664 | tf_op jit(solution)/shard_map/all_gather | solution.py:674
  24.1 7.6 %copy-start.2 = (bf16[256,640]{1,0:T(8,128)(2,1)S(1)}, bf16[256,640]{1,0:T(8,128)(2,1)}, u32[]{:S(2)}) copy-start(bf16[256,640]{1,0:T(8,128)(2,1)} %param.9) | copy-start | bytes 983044
  24.1 9.8 %copy-start.19 = (s32[256]{0:T(256)S(1)}, s32[256]{0:T(256)}, u32[]{:S(2)}) copy-start(s32[256]{0:T(256)} %param.11) | copy-start | bytes 3076
  24.2 4.8 %collective-permute-start.5 = (bf16[4,208,128]{2,1,0:T(8,128)(2,1)S(1)}, bf16[4,208,128]{2,1,0:T(8,128)(2,1)S(1)}, u32[]{:S(2)}, u32[]{:S(2)}) collective-permute-start(bf16[4,208,128]{2,1,0:T(8,128)(2,1)S(1)} %get-tuple-element.106), channel_id=1, source_target_pairs={{0,16},{4,20},{8,24},{12,28},{16,0},{20,4},{24,8},{28,12},{1,17},{... | collective-permute-start | bytes 638984 | tf_op jit(solution)/shard_map/ppermute | solution.py:506
  25.5 5.1 %collective-permute-start.2 = (bf16[4,208,128]{2,1,0:T(8,128)(2,1)S(1)}, bf16[4,208,128]{2,1,0:T(8,128)(2,1)S(1)}, u32[]{:S(2)}, u32[]{:S(2)}) collective-permute-start(bf16[4,208,128]{2,1,0:T(8,128)(2,1)S(1)} %get-tuple-element.107), channel_id=1, source_target_pairs={{0,8},{4,12},{8,0},{12,4},{16,24},{20,28},{24,16},{28,20},{1,9},{5... | collective-permute-start | bytes 638984 | tf_op jit(solution)/shard_map/ppermute | solution.py:506
  29.0 11.8 %collective-permute-start.6 = (bf16[2,4,208,128]{3,2,1,0:T(8,128)(2,1)S(1)}, bf16[2,4,208,128]{3,2,1,0:T(8,128)(2,1)S(1)}, u32[]{:S(2)}, u32[]{:S(2)}) collective-permute-start(bf16[2,4,208,128]{3,2,1,0:T(8,128)(2,1)S(1)} %get-tuple-element.103), channel_id=1, source_target_pairs={{0,8},{4,12},{8,0},{12,4},{16,24},{20,28},{24,16},{28,20},{1,9},{5... | collective-permute-start | bytes 1277960 | tf_op jit(solution)/shard_map/ppermute | solution.py:506
  30.7 14.3 %collective-permute-start.3 = (bf16[2,4,208,128]{3,2,1,0:T(8,128)(2,1)S(1)}, bf16[2,4,208,128]{3,2,1,0:T(8,128)(2,1)S(1)}, u32[]{:S(2)}, u32[]{:S(2)}) collective-permute-start(bf16[2,4,208,128]{3,2,1,0:T(8,128)(2,1)S(1)} %get-tuple-element.109), channel_id=1, source_target_pairs={{0,16},{4,20},{8,24},{12,28},{16,0},{20,4},{24,8},{28,12},{1,17},{... | collective-permute-start | bytes 1277960 | tf_op jit(solution)/shard_map/ppermute | solution.py:506
  31.7 16.0 %collective-permute-start = (bf16[256,640]{1,0:T(8,128)(2,1)S(1)}, bf16[256,640]{1,0:T(8,128)(2,1)S(1)}, u32[]{:S(2)}, u32[]{:S(2)}) collective-permute-start(bf16[256,640]{1,0:T(8,128)(2,1)S(1)} %copy-done.2), channel_id=1, source_target_pairs={{0,1},{1,2},{2,3},{4,5},{5,6},{6,7},{8,9},{9,10},{10,11},{12,13},{... | collective-permute-start | bytes 983048 | tf_op jit(solution)/shard_map/ppermute | solution.py:33
  40.9 18.2 %copy-start = (bf16[2,2,4,208,128]{4,3,2,1,0:T(8,128)(2,1)}, bf16[2,2,4,208,128]{4,3,2,1,0:T(8,128)(2,1)S(1)}, u32[]{:S(2)}) copy-start(bf16[2,2,4,208,128]{4,3,2,1,0:T(8,128)(2,1)S(1)} %pad_maximum_fusion.2) | copy-start | bytes 2555908
  41.0 18.3 %collective-permute-start.7 = (bf16[16,208,128]{2,1,0:T(8,128)(2,1)S(1)}, bf16[16,208,128]{2,1,0:T(8,128)(2,1)S(1)}, u32[]{:S(2)}, u32[]{:S(2)}) collective-permute-start(bf16[16,208,128]{2,1,0:T(8,128)(2,1)S(1)} %bitcast.131), channel_id=1, source_target_pairs={{0,4},{4,0},{8,12},{12,8},{16,20},{20,16},{24,28},{28,24},{1,5},{5... | collective-permute-start | bytes 2555912 | tf_op jit(solution)/shard_map/ppermute | solution.py:506
  45.1 15.1 %copy-start.1 = (bf16[2,2,4,208,128]{4,3,2,1,0:T(8,128)(2,1)}, bf16[2,2,4,208,128]{4,3,2,1,0:T(8,128)(2,1)S(1)}, u32[]{:S(2)}) copy-start(bf16[2,2,4,208,128]{4,3,2,1,0:T(8,128)(2,1)S(1)} %pad_maximum_fusion.1) | copy-start | bytes 2555908
  45.1 15.1 %collective-permute-start.4 = (bf16[16,208,128]{2,1,0:T(8,128)(2,1)S(1)}, bf16[16,208,128]{2,1,0:T(8,128)(2,1)}, u32[]{:S(2)}, u32[]{:S(2)}) collective-permute-start(bf16[16,208,128]{2,1,0:T(8,128)(2,1)S(1)} %bitcast.133), channel_id=1, source_target_pairs={{0,4},{4,0},{8,12},{12,8},{16,20},{20,16},{24,28},{28,24},{1,5},{5... | collective-permute-start | bytes 2555912 | tf_op jit(solution)/shard_map/ppermute | solution.py:506
  47.7 11.4 %collective-permute-start.1 = (bf16[256,640]{1,0:T(8,128)(2,1)S(1)}, bf16[256,640]{1,0:T(8,128)(2,1)S(1)}, u32[]{:S(2)}, u32[]{:S(2)}) collective-permute-start(bf16[256,640]{1,0:T(8,128)(2,1)S(1)} %collective-permute-done), channel_id=1, source_target_pairs={{0,1},{1,2},{2,3},{4,5},{5,6},{6,7},{8,9},{9,10},{10,11},{12,13},{... | collective-permute-start | bytes 983048 | tf_op jit(solution)/shard_map/ppermute | solution.py:33
  59.2 1.0 copy-start.18
  60.2 0.9 copy-start.6
  124.0 40.8 %collective-permute-start.18 = (bf16[16,480,128]{2,1,0:T(8,128)(2,1)}, bf16[16,480,128]{2,1,0:T(8,128)(2,1)}, u32[]{:S(2)}, u32[]{:S(2)}) collective-permute-start(bf16[16,480,128]{2,1,0:T(8,128)(2,1)} %get-tuple-element.83), channel_id=1, source_target_pairs={{0,4},{4,0},{8,12},{12,8},{16,20},{20,16},{24,28},{28,24},{1,5},{5... | collective-permute-start | bytes 5898248 | tf_op jit(solution)/shard_map/ppermute | solution.py:506
  138.2 9.5 %collective-permute-start.8 = (bf16[256,512]{1,0:T(8,128)(2,1)S(1)}, bf16[256,512]{1,0:T(8,128)(2,1)S(1)}, u32[]{:S(2)}, u32[]{:S(2)}) collective-permute-start(bf16[256,512]{1,0:T(8,128)(2,1)S(1)} %slice.72), channel_id=1, source_target_pairs={{1,0},{2,1},{3,2},{5,4},{6,5},{7,6},{9,8},{10,9},{11,10},{13,12},{... | collective-permute-start | bytes 786440 | tf_op jit(solution)/shard_map/ppermute | solution.py:33
  139.5 27.3 %collective-permute-start.20 = (bf16[16,496,128]{2,1,0:T(8,128)(2,1)}, bf16[16,496,128]{2,1,0:T(8,128)(2,1)}, u32[]{:S(2)}, u32[]{:S(2)}) collective-permute-start(bf16[16,496,128]{2,1,0:T(8,128)(2,1)} %get-tuple-element.85), channel_id=1, source_target_pairs={{0,4},{4,0},{8,12},{12,8},{16,20},{20,16},{24,28},{28,24},{1,5},{5... | collective-permute-start | bytes 6094856 | tf_op jit(solution)/shard_map/ppermute | solution.py:506
  147.8 13.5 %collective-permute-start.9 = (bf16[256,512]{1,0:T(8,128)(2,1)S(1)}, bf16[256,512]{1,0:T(8,128)(2,1)S(1)}, u32[]{:S(2)}, u32[]{:S(2)}) collective-permute-start(bf16[256,512]{1,0:T(8,128)(2,1)S(1)} %add_convert_fusion.9), channel_id=1, source_target_pairs={{1,0},{2,1},{3,2},{5,4},{6,5},{7,6},{9,8},{10,9},{11,10},{13,12},{... | collective-permute-start | bytes 786440 | tf_op jit(solution)/shard_map/ppermute | solution.py:33
  149.3 12.1 %copy-start.15 = (bf16[640,256]{1,0:T(8,128)(2,1)S(1)}, bf16[640,256]{1,0:T(8,128)(2,1)}, u32[]{:S(2)}) copy-start(bf16[640,256]{1,0:T(8,128)(2,1)} %get-tuple-element.52.w_k) | copy-start | bytes 983044
  160.0 1.7 copy-start.11
  160.0 1.7 copy-start.14
  160.0 3.4 %collective-permute-start.10 = (bf16[16,208,128]{2,1,0:T(8,128)(2,1)}, bf16[16,208,128]{2,1,0:T(8,128)(2,1)S(1)}, u32[]{:S(2)}, u32[]{:S(2)}) collective-permute-start(bf16[16,208,128]{2,1,0:T(8,128)(2,1)} %get-tuple-element.79), channel_id=1, source_target_pairs={{0,4},{4,0},{8,12},{12,8},{16,20},{20,16},{24,28},{28,24},{1,5},{5... | collective-permute-start | bytes 2555912 | tf_op jit(solution)/shard_map/ppermute | solution.py:506
  161.2 8.0 %collective-permute-start.13 = (bf16[16,208,128]{2,1,0:T(8,128)(2,1)}, bf16[16,208,128]{2,1,0:T(8,128)(2,1)S(1)}, u32[]{:S(2)}, u32[]{:S(2)}) collective-permute-start(bf16[16,208,128]{2,1,0:T(8,128)(2,1)} %get-tuple-element.81), channel_id=1, source_target_pairs={{0,4},{4,0},{8,12},{12,8},{16,20},{20,16},{24,28},{28,24},{1,5},{5... | collective-permute-start | bytes 2555912 | tf_op jit(solution)/shard_map/ppermute | solution.py:506
  161.4 2.1 copy-start.8
  161.7 3.1 %copy-start.5 = (bf16[16,480,128]{2,1,0:T(8,128)(2,1)S(1)}, bf16[16,480,128]{2,1,0:T(8,128)(2,1)}, u32[]{:S(2)}) copy-start(bf16[16,480,128]{2,1,0:T(8,128)(2,1)} %get-tuple-element.82) | copy-start | bytes 5898244
  163.5 3.4 %copy-start.3 = (bf16[16,496,128]{2,1,0:T(8,128)(2,1)S(1)}, bf16[16,496,128]{2,1,0:T(8,128)(2,1)}, u32[]{:S(2)}) copy-start(bf16[16,496,128]{2,1,0:T(8,128)(2,1)} %get-tuple-element.84) | copy-start | bytes 6094852
  163.6 11.1 %collective-permute-start.11 = (bf16[2,4,208,128]{3,2,1,0:T(8,128)(2,1)S(1)}, bf16[2,4,208,128]{3,2,1,0:T(8,128)(2,1)S(1)}, u32[]{:S(2)}, u32[]{:S(2)}) collective-permute-start(bf16[2,4,208,128]{3,2,1,0:T(8,128)(2,1)S(1)} %fusion.20), channel_id=1, source_target_pairs={{0,16},{4,20},{8,24},{12,28},{16,0},{20,4},{24,8},{28,12},{1,17},{... | collective-permute-start | bytes 1277960 | tf_op jit(solution)/shard_map/ppermute | solution.py:506
  166.4 2.9 %copy-start.7 = (bf16[16,208,128]{2,1,0:T(8,128)(2,1)S(1)}, bf16[16,208,128]{2,1,0:T(8,128)(2,1)}, u32[]{:S(2)}) copy-start(bf16[16,208,128]{2,1,0:T(8,128)(2,1)} %get-tuple-element.80) | copy-start | bytes 2555908
  166.4 35.6 %collective-permute-start.19 = (bf16[2,4,480,128]{3,2,1,0:T(8,128)(2,1)S(1)}, bf16[2,4,480,128]{3,2,1,0:T(8,128)(2,1)S(1)}, u32[]{:S(2)}, u32[]{:S(2)}) collective-permute-start(bf16[2,4,480,128]{3,2,1,0:T(8,128)(2,1)S(1)} %fusion.7), channel_id=1, source_target_pairs={{0,16},{4,20},{8,24},{12,28},{16,0},{20,4},{24,8},{28,12},{1,17},{... | collective-permute-start | bytes 2949128 | tf_op jit(solution)/shard_map/ppermute | solution.py:506
  168.3 33.6 %collective-permute-start.21 = (bf16[2,4,496,128]{3,2,1,0:T(8,128)(2,1)S(1)}, bf16[2,4,496,128]{3,2,1,0:T(8,128)(2,1)S(1)}, u32[]{:S(2)}, u32[]{:S(2)}) collective-permute-start(bf16[2,4,496,128]{3,2,1,0:T(8,128)(2,1)S(1)} %fusion.2), channel_id=1, source_target_pairs={{0,8},{4,12},{8,0},{12,4},{16,24},{20,28},{24,16},{28,20},{1,9},{5... | collective-permute-start | bytes 3047432 | tf_op jit(solution)/shard_map/ppermute | solution.py:506
  169.3 31.4 %collective-permute-start.14 = (bf16[2,4,208,128]{3,2,1,0:T(8,128)(2,1)S(1)}, bf16[2,4,208,128]{3,2,1,0:T(8,128)(2,1)S(1)}, u32[]{:S(2)}, u32[]{:S(2)}) collective-permute-start(bf16[2,4,208,128]{3,2,1,0:T(8,128)(2,1)S(1)} %fusion.22), channel_id=1, source_target_pairs={{0,8},{4,12},{8,0},{12,4},{16,24},{20,28},{24,16},{28,20},{1,9},{5... | collective-permute-start | bytes 1277960 | tf_op jit(solution)/shard_map/ppermute | solution.py:506
  174.8 31.8 %collective-permute-start.12 = (bf16[4,208,128]{2,1,0:T(8,128)(2,1)S(1)}, bf16[4,208,128]{2,1,0:T(8,128)(2,1)S(1)}, u32[]{:S(2)}, u32[]{:S(2)}) collective-permute-start(bf16[4,208,128]{2,1,0:T(8,128)(2,1)S(1)} %dynamic-slice_bitcast_fusion.5), channel_id=1, source_target_pairs={{0,8},{4,12},{8,0},{12,4},{16,24},{20,28},{24,16},{28,20},{1,9},{5... | collective-permute-start | bytes 638984 | tf_op jit(solution)/shard_map/ppermute | solution.py:506
  201.0 5.7 %collective-permute-start.15 = (bf16[4,208,128]{2,1,0:T(8,128)(2,1)S(1)}, bf16[4,208,128]{2,1,0:T(8,128)(2,1)S(1)}, u32[]{:S(2)}, u32[]{:S(2)}) collective-permute-start(bf16[4,208,128]{2,1,0:T(8,128)(2,1)S(1)} %dynamic-slice_bitcast_fusion.4), channel_id=1, source_target_pairs={{0,16},{4,20},{8,24},{12,28},{16,0},{20,4},{24,8},{28,12},{1,17},{... | collective-permute-start | bytes 638984 | tf_op jit(solution)/shard_map/ppermute | solution.py:506
  203.6 13.0 %collective-permute-start.23 = (bf16[4,496,128]{2,1,0:T(8,128)(2,1)S(1)}, bf16[4,496,128]{2,1,0:T(8,128)(2,1)S(1)}, u32[]{:S(2)}, u32[]{:S(2)}) collective-permute-start(bf16[4,496,128]{2,1,0:T(8,128)(2,1)S(1)} %dynamic-slice_bitcast_fusion), channel_id=1, source_target_pairs={{0,16},{4,20},{8,24},{12,28},{16,0},{20,4},{24,8},{28,12},{1,17},{... | collective-permute-start | bytes 1523720 | tf_op jit(solution)/shard_map/ppermute | solution.py:506
  206.0 9.4 %collective-permute-start.22 = (bf16[4,480,128]{2,1,0:T(8,128)(2,1)S(1)}, bf16[4,480,128]{2,1,0:T(8,128)(2,1)S(1)}, u32[]{:S(2)}, u32[]{:S(2)}) collective-permute-start(bf16[4,480,128]{2,1,0:T(8,128)(2,1)S(1)} %dynamic-slice_bitcast_fusion.2), channel_id=1, source_target_pairs={{0,8},{4,12},{8,0},{12,4},{16,24},{20,28},{24,16},{28,20},{1,9},{5... | collective-permute-start | bytes 1474568 | tf_op jit(solution)/shard_map/ppermute | solution.py:506
  206.9 13.6 %collective-permute-start.16 = (bf16[2,416,128]{2,1,0:T(8,128)(2,1)S(1)}, bf16[2,416,128]{2,1,0:T(8,128)(2,1)S(1)}, u32[]{:S(2)}, u32[]{:S(2)}) collective-permute-start(bf16[2,416,128]{2,1,0:T(8,128)(2,1)S(1)} %dynamic-slice_bitcast_fusion.3), channel_id=1, source_target_pairs={{0,1},{1,0},{2,3},{3,2},{4,5},{5,4},{6,7},{7,6},{8,9},{9,8},{10,11... | collective-permute-start | bytes 638984 | tf_op jit(solution)/shard_map/ppermute | solution.py:533
  216.7 2.7 %copy-start.10 = (f32[256,640]{1,0:T(8,128)S(1)}, f32[256,640]{1,0:T(8,128)}, u32[]{:S(2)}) copy-start(f32[256,640]{1,0:T(8,128)} %get-tuple-element.60.grad_middle) | copy-start | bytes 1966084
  217.0 13.1 %collective-permute-start.24 = (bf16[2,976,128]{2,1,0:T(8,128)(2,1)S(1)}, bf16[2,976,128]{2,1,0:T(8,128)(2,1)S(1)}, u32[]{:S(2)}, u32[]{:S(2)}) collective-permute-start(bf16[2,976,128]{2,1,0:T(8,128)(2,1)S(1)} %dynamic-slice_bitcast_fusion.1), channel_id=1, source_target_pairs={{0,1},{1,0},{2,3},{3,2},{4,5},{5,4},{6,7},{7,6},{8,9},{9,8},{10,11... | collective-permute-start | bytes 1499144 | tf_op jit(solution)/shard_map/ppermute | solution.py:533
  220.5 11.2 %copy-start.9 = (f32[401,128]{1,0:T(8,128)S(1)}, f32[401,128]{1,0:T(8,128)}, u32[]{:S(2)}) copy-start(f32[401,128]{1,0:T(8,128)} %param.12) | copy-start | bytes 615940
  220.5 11.2 %copy-start.16 = (f32[401,128]{1,0:T(8,128)S(1)}, f32[401,128]{1,0:T(8,128)}, u32[]{:S(2)}) copy-start(f32[401,128]{1,0:T(8,128)} %param.14) | copy-start | bytes 615940
  220.5 11.2 %copy-start.17 = (f32[401,128]{1,0:T(8,128)S(1)}, f32[401,128]{1,0:T(8,128)}, u32[]{:S(2)}) copy-start(f32[401,128]{1,0:T(8,128)} %param.15) | copy-start | bytes 615940
  220.6 24.5 %copy-start.4 = (f32[961,128]{1,0:T(8,128)S(1)}, f32[961,128]{1,0:T(8,128)}, u32[]{:S(2)}) copy-start(f32[961,128]{1,0:T(8,128)} %param.13) | copy-start | bytes 1476100
  220.6 24.5 %copy-start.12 = (f32[961,128]{1,0:T(8,128)S(1)}, f32[961,128]{1,0:T(8,128)}, u32[]{:S(2)}) copy-start(f32[961,128]{1,0:T(8,128)} %param.16) | copy-start | bytes 1476100
  220.6 24.5 %copy-start.13 = (f32[961,128]{1,0:T(8,128)S(1)}, f32[961,128]{1,0:T(8,128)}, u32[]{:S(2)}) copy-start(f32[961,128]{1,0:T(8,128)} %param.17) | copy-start | bytes 1476100
  220.7 11.1 %collective-permute-start.17 = (bf16[1,416,128]{2,1,0:T(8,128)(2,1)S(1)}, bf16[1,416,128]{2,1,0:T(8,128)(2,1)S(1)}, u32[]{:S(2)}, u32[]{:S(2)}) collective-permute-start(bf16[1,416,128]{2,1,0:T(8,128)(2,1)S(1)} %constant_dynamic-slice_fusion), channel_id=1, source_target_pairs={{0,2},{1,3},{2,0},{3,1},{4,6},{5,7},{6,4},{7,5},{8,10},{9,11},{10,... | collective-permute-start | bytes 319496 | tf_op jit(solution)/shard_map/ppermute | solution.py:533
  230.3 14.8 %collective-permute-start.25 = (bf16[1,976,128]{2,1,0:T(8,128)(2,1)S(1)}, bf16[1,976,128]{2,1,0:T(8,128)(2,1)S(1)}, u32[]{:S(2)}, u32[]{:S(2)}) collective-permute-start(bf16[1,976,128]{2,1,0:T(8,128)(2,1)S(1)} %constant_dynamic-slice_fusion.1), channel_id=1, source_target_pairs={{0,2},{1,3},{2,0},{3,1},{4,6},{5,7},{6,4},{7,5},{8,10},{9,11},{10,... | collective-permute-start | bytes 749576 | tf_op jit(solution)/shard_map/ppermute | solution.py:533
Sparse Core Ops, SparseCore 0:
  11.5 80.3 all-gather.4
